TPU v7x, 32 devices: a whole 2x2x4 slice. The times are simulated.
32 devices in a mesh: chan: 8 (over z, y), pair: 4 (over x, core).
Axes of the slice: x: 2, y: 2, z: 4, core: 2. Of those that a mesh axis runs over, the one named last changes fastest.
Arguments:
- voltages: bfloat16 [4, 16, 2, 34560], P('pair', 'chan'), may hold values from -6 to 6
- fir_taps: float32 [8, 256], replicated, may hold values from -2 to 2
Outputs:
- visibilities: float32 [128, 2, 64, 64], P('chan', None, 'pair')
All inputs are finite; a program needn't handle non-finite values.
Results may differ from a plain program's by a relative error of at most 0.0036.
Values may be sent and summed in bfloat16 or wider, within the bound.
No kernel may reach another device: no remote copies, remote signals or barrier semaphores. Data moves between devices by JAX's collectives and lax.ppermute only.
A program may use at most 64 MiB of HBM per device.

v0:
```python
import math

import jax
import jax.numpy as jnp
from jax import lax
from jax.sharding import PartitionSpec as P


def dft_rows(channels):
    frame = 2 * channels
    row_index = jnp.arange(2 * channels, dtype=jnp.int32)
    col_index = jnp.arange(frame, dtype=jnp.int32)
    freq_index = row_index // 2
    phases = freq_index[:, None] * col_index[None, :] % frame
    angles = phases.astype(jnp.float32) * (2.0 * math.pi / frame)
    chosen = jnp.where((row_index % 2 == 0)[:, None], jnp.cos(angles), -jnp.sin(angles))
    return chosen * (1.0 / math.sqrt(frame))


def channelize(sample_rows, fir_taps, transform, spectra_len):
    tap_count, frame = fir_taps.shape
    channels = frame // 2
    framed = sample_rows.astype(jnp.float32).reshape(
        sample_rows.shape[0], spectra_len + tap_count - 1, frame
    )
    filtered = jnp.zeros((sample_rows.shape[0], spectra_len, frame), jnp.float32)
    for tap in range(tap_count):
        filtered = filtered + fir_taps[tap][None, None, :] * framed[:, tap : tap + spectra_len, :]
    spectra = jnp.einsum("wn,asn->aws", transform, filtered, precision=lax.Precision.HIGHEST)
    return spectra.reshape(sample_rows.shape[0], channels, 2 * spectra_len).astype(jnp.bfloat16)


def correlate(own_rows, columns, spectra_len):
    blocks = columns.shape[2] // (2 * spectra_len)
    shaped = columns.reshape(columns.shape[0], columns.shape[1], blocks, 2, spectra_len)
    rotated = jnp.stack([-shaped[:, :, :, 1, :], shaped[:, :, :, 0, :]], axis=3).reshape(
        columns.shape
    )
    stacked = jnp.concatenate([columns, rotated], axis=0)
    stacked = jnp.transpose(stacked, (1, 0, 2))
    own_first = jnp.transpose(own_rows, (1, 0, 2))
    product = jnp.einsum("cik,cjk->cij", own_first, stacked, preferred_element_type=jnp.float32)
    count = columns.shape[0]
    product = product.reshape(product.shape[0], product.shape[1], 2, count)
    return jnp.transpose(product, (0, 2, 1, 3))


def shards(voltages, fir_taps):
    samples = voltages[0]
    batch_count = samples.shape[1]
    tap_count, frame = fir_taps.shape
    spectra_len = samples.shape[2] // frame - tap_count + 1
    transform = dft_rows(frame // 2)
    pieces = [
        channelize(samples[:, batch], fir_taps, transform, spectra_len)
        for batch in range(batch_count)
    ]
    spectra = jnp.concatenate(pieces, axis=2)[None]
    turned = lax.all_to_all(spectra, "chan", split_axis=2, concat_axis=1, tiled=True)
    own_rows = turned[0]
    arrived = lax.all_gather(turned, "pair", axis=0, tiled=True)
    flat = arrived.reshape(arrived.shape[0] * arrived.shape[1], arrived.shape[2], arrived.shape[3])
    summed = correlate(own_rows, flat, spectra_len)
    return summed * (1.0 / math.sqrt(batch_count * spectra_len))


def solution(mesh):
    in_specs = (P("pair", "chan", None, None), P())
    out_specs = P("chan", None, "pair", None)
    return jax.shard_map(shards, mesh=mesh, in_specs=in_specs, out_specs=out_specs, check_vma=False)
```

profile of v0, /device:TPU:0, one launch (start us, length us, event | category | flops | bytes accessed | tf_op | source)
XLA Modules:
  0.0 65.0 jit_solution(2341271604149292192)
XLA Ops:
  6.5 0.0 all-gather.2.cloned.1.call-start
  6.5 1.0 %fusion.75 = (f32[1,256]{1,0:T(1,128)S(1)}, f32[1,256]{1,0:T(1,128)S(1)}, f32[1,256]{1,0:T(1,128)S(1)}, f32[1,256]{1,0:T(1,128)S(1)}, f32[1,256]{1,0:T(1,128)S(1...) fusion(f32[8,256]{1,0:T(8,128)} %param.3), kind=kLoop, calls=%fused_computation.95 | loop fusion | bytes 16384 | tf_op jit(solution)/shard_map/slice | solution.py:28
  7.5 2.8 %fusion.7 = (f32[2,34560]{1,0:T(2,128)S(1)}, f32[2,34560]{1,0:T(2,128)S(1)}) fusion(bf16[2,2,34560]{2,1,0:T(2,128)(2,1)} %bitcast.44), kind=kLoop, calls=%fused_computation.17 | loop fusion | flops 138240 | bytes 829440 | tf_op jit(solution)/shard_map/convert_element_type | solution.py:23
  10.4 0.2 reshape.55
  10.6 1.7 %fusion.3 = bf16[2,256,128]{1,2,0:T(8,128)(2,1)S(1)} fusion(f32[2,135,256]{2,1,0:T(8,128)S(1)} %reshape.55, f32[256]{0:T(256)S(1)} %bitcast.59, f32[256]{0:T(256)S(1)} %bitcast.61, f32[256]{0:T(256)S(1)} %bitcast.49, f32[256]{0:T(256)S(1)} %bitcast.51, f32[256]{0:T(256)S(1)} %bitcast.53, f32[256]{0:T(256)S(1)} %bitcast.55, f32[256]{0:T(256)S(1)} %bitcast.57, ...), kind=kOutput, calls=%fused_computation.6 | convolution fusion | flops 203489280 | bytes 2237952 | tf_op jit(solution)/shard_map/wn,asn->aws/dot_general | solution.py:29
  12.4 0.1 copy.16
  12.6 0.2 reshape.56
  12.8 1.7 %fusion.4 = bf16[2,256,128]{1,2,0:T(8,128)(2,1)S(1)} fusion(f32[2,135,256]{2,1,0:T(8,128)S(1)} %reshape.56, f32[256]{0:T(256)S(1)} %bitcast.60, f32[256]{0:T(256)S(1)} %bitcast.62, f32[256]{0:T(256)S(1)} %bitcast.50, f32[256]{0:T(256)S(1)} %bitcast.52, f32[256]{0:T(256)S(1)} %bitcast.54, f32[256]{0:T(256)S(1)} %bitcast.56, f32[256]{0:T(256)S(1)} %bitcast.58, ...), kind=kOutput, calls=%fused_computation.7 | convolution fusion | flops 203489280 | bytes 2237952 | tf_op jit(solution)/shard_map/wn,asn->aws/dot_general | solution.py:29
  14.5 0.1 copy.17
  14.8 0.3 copy.18
  15.0 16.0 %all_to_all.18 = bf16[1,2,128,512]{3,1,0,2:T(2,128)(2,1)S(1)} all-to-all(bf16[1,2,128,512]{3,1,0,2:T(2,128)(2,1)S(1)} %copy.18), channel_id=1, replica_groups=mesh['chan'=8,'pair'=4] {'chan'}, dimensions={2} | all-to-all | bytes 524288 | tf_op jit(solution)/shard_map/all_to_all | solution.py:59
  31.1 0.7 %copy.21 = bf16[1,8,2,16,512]{4,3,2,1,0:T(8,128)(2,1)} copy(bf16[1,8,2,16,512]{4,3,1,2,0:T(8,128)(2,1)S(1)} %bitcast.42) | data formatting | bytes 524288 | tf_op jit(solution)/shard_map/all_to_all | solution.py:59
  31.8 0.0 all-gather.2.cloned.1.call-update
  31.8 0.3 copy.20
  32.1 0.1 squeeze.10
  32.2 15.5 %all-gather.2.cloned.1.call-done = bf16[4,16,16,512]{3,2,1,0:T(8,128)(2,1)} async-done(((bf16[1,16,16,512]{3,2,1,0:T(8,128)(2,1)}), bf16[4,16,16,512]{3,2,1,0:T(8,128)(2,1)}) %all-gather.2.cloned.1.call-update) | async-done | bytes 1048592 | tf_op jit(solution)/shard_map/all_gather | solution.py:61
  47.7 1.3 %reshape_reshape.3 = bf16[64,16,2,2,128]{4,3,2,1,0:T(2,128)(2,1)S(1)} reshape(bf16[4,16,16,512]{3,2,1,0:T(8,128)(2,1)} %all-gather.2.cloned.1.call-done) | data formatting | bytes 2097152 | tf_op jit(solution)/shard_map/reshape;reshape | solution.py:35
  49.0 2.4 %fusion.74 = (bf16[64,16,2,1,128]{4,3,2,1,0:T(2,128)(2,1)S(1)}, bf16[64,16,2,1,128]{4,3,2,1,0:T(2,128)(2,1)S(1)}) fusion(bf16[64,16,2,2,128]{4,3,2,1,0:T(2,128)(2,1)S(1)} %reshape_reshape.3), kind=kLoop, calls=%fused_computation.94 | loop fusion | bytes 2097152 | tf_op jit(solution)/shard_map/slice | solution.py:36
  51.4 1.1 %copy_negate_fusion = bf16[64,16,2,1,128]{4,3,2,0,1:T(2,128)(2,1)S(1)} fusion(bf16[64,16,2,1,128]{4,3,2,1,0:T(2,128)(2,1)S(1)} %get-tuple-element.7), kind=kLoop, calls=%fused_computation.10 | loop fusion | flops 262144 | bytes 1048576 | tf_op jit(solution)/shard_map/neg | solution.py:36
  52.5 2.2 %pad_maximum_fusion = bf16[64,16,2,2,128]{4,3,2,0,1:T(2,128)(2,1)S(1)} fusion(bf16[64,16,2,1,128]{4,3,2,0,1:T(2,128)(2,1)S(1)} %copy_negate_fusion, bf16[64,16,2,1,128]{4,3,2,1,0:T(2,128)(2,1)S(1)} %get-tuple-element.8), kind=kLoop, calls=%fused_computation.9 | loop fusion | flops 2097152 | bytes 2097152 | tf_op jit(solution)/shard_map/stack | solution.py:36
  54.7 0.0 copy-start
  54.8 0.4 reshape.54
  55.2 0.8 %copy-done = bf16[4,16,16,512]{3,2,1,0:T(8,128)(2,1)S(1)} copy-done((bf16[4,16,16,512]{3,2,1,0:T(8,128)(2,1)S(1)}, bf16[4,16,16,512]{3,2,1,0:T(8,128)(2,1)}, u32[]{:S(2)}) %copy-start) | copy-done | bytes 1048600
  56.0 0.6 copy.22
  56.6 0.7 %fusion.5 = f32[16,16,128]{2,1,0:T(8,128)S(1)} fusion(bf16[64,16,512]{2,0,1:T(8,128)(2,1)S(1)} %reshape.54, bf16[64,16,512]{2,0,1:T(8,128)(2,1)S(1)} %bitcast.45, bf16[16,16,512]{2,0,1:T(8,128)(2,1)S(1)} %squeeze.10), kind=kOutput, calls=%fused_computation.8 | convolution fusion | flops 37781504 | bytes 2490368 | tf_op jit(solution)/shard_map/cik,cjk->cij/dot_general | solution.py:42
  57.2 0.2 mul.216
  57.4 0.7 %copy.32 = f32[16,16,2,64]{3,1,2,0:T(8,128)} copy(f32[16,16,2,64]{3,2,1,0:T(2,128)S(1)} %mul.216) | data formatting | bytes 262144 | tf_op jit(solution)/shard_map/mul | solution.py:64
  (6 shorter events, 0.2 us)
Async XLA Ops:
  6.5 41.2 %all-gather.2.cloned.1.call-start = ((), (), s32[]{:S(2)}) async-start(), calls=%async_computation.1 | async-start | bytes 1310720 | tf_op jit(solution)/shard_map/all_gather | solution.py:61
  54.7 1.2 %copy-start = (bf16[4,16,16,512]{3,2,1,0:T(8,128)(2,1)S(1)}, bf16[4,16,16,512]{3,2,1,0:T(8,128)(2,1)}, u32[]{:S(2)}) copy-start(bf16[4,16,16,512]{3,2,1,0:T(8,128)(2,1)} %all-gather.2.cloned.1.call-done) | copy-start | bytes 3145732
Sparse Core Ops, SparseCore 0:
  32.0 15.6 all-gather.1
where the time goes:
time: 65.3 us; the launch traced here: 65 us
  blocking collectives  16 us (25%)
  waiting for transfers between devices  15.5 us (24%)
  between operations  13.5 us (21%)
  local copies, waits for them, and re-layouts  9.59 us (15%)
  other arithmetic  6.2 us (9%)
  matrix products  4.15 us (6%)
    all_to_all x1, blocking collectives, shards(): lax.all_to_all(spectra, 'chan', split_axis=2, concat_axis=1, tiled=True)  16 us
    all_gather x1, waiting for transfers between devices, shards(): arrived = lax.all_gather(turned, 'pair', axis=0, tiled=True)  15.5 us
    dot_general x2, matrix products, channelize(): jnp.einsum('wn,asn->aws', transform, filtered, precision=lax.Precision.HI...  3.49 us
    convert_element_type x1, other arithmetic, channelize(): sample_rows.astype(jnp.float32)  2.85 us
    slice x1, local copies, waits for them, and re-layouts, correlate(): shaped[:, :, :, 1, :]  2.36 us
    another operation x1, other arithmetic, correlate(): jnp.stack([-shaped[:, :, :, 1, :], shaped[:, :, :, 0, :]], axis=3)  2.22 us
    another operation x1, local copies, waits for them, and re-layouts, correlate(): columns.reshape(columns.shape[0], columns.shape[1], blocks, 2, spectra_len)  1.34 us
  transfers between devices with their start and end apart: 1, of which 1 were waited for; matrix products, arithmetic and copies ran while one was open for 1% of the time, Pallas kernels for 0%

commit v1 on v0

--- a/solution.py
+++ b/solution.py
@@ -1,9 +1,16 @@
+import functools
 import math
 
 import jax
 import jax.numpy as jnp
+import numpy as np
 from jax import lax
+from jax.experimental import pallas as pl
+from jax.experimental.pallas import tpu as pltpu
 from jax.sharding import PartitionSpec as P
+
+LANES = 128
+VMEM = pltpu.MemorySpace.VMEM
 
 
 def dft_rows(channels):
@@ -15,6 +22,15 @@
     angles = phases.astype(jnp.float32) * (2.0 * math.pi / frame)
     chosen = jnp.where((row_index % 2 == 0)[:, None], jnp.cos(angles), -jnp.sin(angles))
     return chosen * (1.0 / math.sqrt(frame))
+
+
+def dft_table(channels):
+    frame = 2 * channels
+    row = np.arange(frame)
+    phases = (row // 2)[:, None] * np.arange(frame)[None, :] % frame
+    angles = phases * (2.0 * np.pi / frame)
+    chosen = np.where((row % 2 == 0)[:, None], np.cos(angles), -np.sin(angles))
+    return chosen / np.sqrt(frame)
 
 
 def channelize(sample_rows, fir_taps, transform, spectra_len):
@@ -45,7 +61,7 @@
     return jnp.transpose(product, (0, 2, 1, 3))
 
 
-def shards(voltages, fir_taps):
+def gathered_shards(voltages, fir_taps):
     samples = voltages[0]
     batch_count = samples.shape[1]
     tap_count, frame = fir_taps.shape
@@ -64,7 +80,151 @@
     return summed * (1.0 / math.sqrt(batch_count * spectra_len))
 
 
+def channelize_kernel(antennas, batches, frames, v_ref, taps_ref, dft_ref, o_ref, x_ref, f_ref):
+    taps, frame = taps_ref.shape
+    parts = frame // LANES
+    step = parts * batches
+    spectra = frames - taps + 1
+    x_ref[...] = v_ref[...].astype(jnp.float32)
+    for a in range(antennas):
+        for b in range(batches):
+            for h in range(parts):
+                lanes = slice(h * LANES, (h + 1) * LANES)
+                total = None
+                for p in range(taps):
+                    first = (a * frames + p) * step + h * batches + b
+                    term = taps_ref[p : p + 1, lanes] * x_ref[pl.ds(first, spectra, stride=step), :]
+                    total = term if total is None else total + term
+                f_ref[a, b * spectra : (b + 1) * spectra, lanes] = total.astype(jnp.bfloat16)
+        spec = lax.dot_general(
+            dft_ref[...], f_ref[a], (((1,), (1,)), ((), ())), preferred_element_type=jnp.float32
+        )
+        o_ref[:, a, :, :] = spec.astype(jnp.bfloat16).reshape(
+            o_ref.shape[0], o_ref.shape[2], o_ref.shape[3]
+        )
+
+
+def correlate_kernel(groups, blocks, antennas, channels, scale, y_ref, *refs):
+    outs, scr, vis = refs[: blocks], refs[blocks], refs[blocks + 1]
+    rows = antennas * channels * 2
+    width = y_ref.shape[1]
+    parts = width // LANES
+    total = groups * blocks * antennas
+    for g in range(groups):
+        for q in range(blocks):
+            src = y_ref[(g * blocks + q) * rows : (g * blocks + q + 1) * rows, :].astype(jnp.float32)
+            for t in range(parts):
+                scr[t, (q * groups + g) * rows : (q * groups + g + 1) * rows, :] = src[
+                    :, t * LANES : (t + 1) * LANES
+                ]
+    for c in range(channels):
+        re = [scr[t, pl.ds(2 * c, total, stride=2 * channels), :] for t in range(parts)]
+        im = [scr[t, pl.ds(2 * c + 1, total, stride=2 * channels), :] for t in range(parts)]
+        own = jnp.concatenate(re + im, axis=1).astype(jnp.bfloat16)
+        turned = jnp.concatenate([-x for x in im] + re, axis=1).astype(jnp.bfloat16)
+        both = jnp.concatenate([own, turned], axis=0)
+        prod = lax.dot_general(
+            own, both, (((1,), (1,)), ((), ())), preferred_element_type=jnp.float32
+        )
+        vis[:, c, :, :] = (prod * scale).reshape(blocks, total // blocks, 2 * total)
+    me = lax.axis_index("pair")
+    for j in range(blocks):
+        outs[j][...] = vis[me ^ j]
+
+
+def place_kernel(blocks, *refs):
+    ins, o_ref = refs[:blocks], refs[blocks]
+    channels = ins[0].shape[0]
+    columns = ins[0].shape[2] // 2
+    me = lax.axis_index("pair")
+    for j in range(blocks):
+        at = pl.ds((me ^ j) * channels, channels)
+        block = ins[j][...]
+        o_ref[at, 0, :, :] = block[:, :, :columns]
+        o_ref[at, 1, :, :] = block[:, :, columns:]
+
+
+def exchanged_shards(groups, blocks, voltages, fir_taps):
+    _, antennas, batches, length = voltages.shape
+    taps, frame = fir_taps.shape
+    frames = length // frame
+    spectra = frames - taps + 1
+    parts = frame // LANES
+    devices = groups * blocks
+    channels = frame // 2 // devices
+    total = devices * antennas
+    rows = antennas * frames * parts * batches
+    lined = voltages.reshape(antennas, batches, frames * parts, LANES)
+    lined = jnp.transpose(lined, (0, 2, 1, 3)).reshape(rows, LANES)
+    table = jnp.asarray(dft_table(frame // 2), jnp.bfloat16)
+    vmem = pl.BlockSpec(memory_space=VMEM)
+    sent = pl.pallas_call(
+        functools.partial(channelize_kernel, antennas, batches, frames),
+        out_shape=jax.ShapeDtypeStruct(
+            (devices, antennas, 2 * channels, batches * spectra), jnp.bfloat16
+        ),
+        in_specs=[vmem] * 3,
+        out_specs=vmem,
+        scratch_shapes=[
+            pltpu.VMEM((rows, LANES), jnp.float32),
+            pltpu.VMEM((antennas, batches * spectra, frame), jnp.bfloat16),
+        ],
+        name="channelize",
+    )(lined, fir_taps, table)
+    sent = sent.reshape(devices, antennas * 2 * channels, batches * spectra)
+    turned = lax.all_to_all(sent, ("chan", "pair"), 0, 0, tiled=True)
+    own_shape = jax.ShapeDtypeStruct((channels, total // blocks, 2 * total), jnp.float32)
+    pieces = pl.pallas_call(
+        functools.partial(
+            correlate_kernel,
+            groups,
+            blocks,
+            antennas,
+            channels,
+            1.0 / math.sqrt(batches * spectra),
+        ),
+        out_shape=[own_shape] * blocks,
+        in_specs=[vmem],
+        out_specs=[vmem] * blocks,
+        scratch_shapes=[
+            pltpu.VMEM(
+                (batches * spectra // LANES, devices * antennas * 2 * channels, LANES), jnp.float32
+            ),
+            pltpu.VMEM((blocks, channels, total // blocks, 2 * total), jnp.float32),
+        ],
+        name="correlate",
+    )(turned.reshape(devices * antennas * 2 * channels, batches * spectra))
+    arrived = [pieces[0]] + [
+        lax.ppermute(pieces[j], "pair", [(i, i ^ j) for i in range(blocks)])
+        for j in range(1, blocks)
+    ]
+    return pl.pallas_call(
+        functools.partial(place_kernel, blocks),
+        out_shape=jax.ShapeDtypeStruct(
+            (blocks * channels, 2, total // blocks, total), jnp.float32
+        ),
+        in_specs=[vmem] * blocks,
+        out_specs=vmem,
+        name="place",
+    )(*arrived)
+
+
 def solution(mesh):
+    groups, blocks = mesh.shape["chan"], mesh.shape["pair"]
     in_specs = (P("pair", "chan", None, None), P())
     out_specs = P("chan", None, "pair", None)
+
+    def shards(voltages, fir_taps):
+        channels = fir_taps.shape[1] // 2
+        spectra = voltages.shape[3] // fir_taps.shape[1] - fir_taps.shape[0] + 1
+        if (
+            channels % (groups * blocks) == 0
+            and blocks & (blocks - 1) == 0
+            and fir_taps.shape[1] % LANES == 0
+            and spectra % LANES == 0
+            and voltages.shape[1] * 2 * channels // (groups * blocks) % 16 == 0
+        ):
+            return exchanged_shards(groups, blocks, voltages, fir_taps)
+        return gathered_shards(voltages, fir_taps)
+
     return jax.shard_map(shards, mesh=mesh, in_specs=in_specs, out_specs=out_specs, check_vma=False)

time: 65.3 us -> 31.6 us (0.48)
  between operations: 13.5 us -> 0.01 us
  waiting for transfers between devices: 15.5 us -> 2.86 us
  local copies, waits for them, and re-layouts: 9.59 us -> 2.67 us
  other arithmetic: 6.2 us -> 0 us
  Pallas kernels: 0 us -> 5.83 us
  matrix products: 4.15 us -> 0 us
  blocking collectives: 16 us -> 18 us
  starting transfers between devices: 0.01 us -> 1.86 us
    all_gather x1 -> x0, waiting for transfers between devices: 15.5 us -> none  [shards(): arrived = lax.all_gather(turned, 'pair', axis=0, tiled=True)]
    pallas_call x0 -> x3, Pallas kernels: none -> 5.83 us  [the longest x1 2.27 us: exchanged_shards(): pl.pallas_call(functools.partial(channelize_kernel, antennas, batches, fr...]
    dot_general x3 -> x0, matrix products: 4.15 us -> none  [the longest x2 3.49 us: channelize(): jnp.einsum('wn,asn->aws', transform, filtered, precision=lax.Precision.HI...]
    slice x2 -> x0, local copies, waits for them, and re-layouts: 3.35 us -> none  [the longest x1 2.36 us: correlate(): shaped[:, :, :, 1, :]]
    ppermute x0 -> x3, waiting for transfers between devices: none -> 2.86 us  [exchanged_shards(): lax.ppermute(pieces[j], 'pair', [(i, i ^ j) for i in range(blocks)])]
    convert_element_type x1 -> x0, other arithmetic: 2.85 us -> none  [channelize(): sample_rows.astype(jnp.float32)]
    another operation x1 -> x0, other arithmetic: 2.22 us -> none  [correlate(): jnp.stack([-shaped[:, :, :, 1, :], shaped[:, :, :, 0, :]], axis=3)]
    all_to_all x1, blocking collectives: 16 us -> 18 us  [exchanged_shards(): turned = lax.all_to_all(sent, ('chan', 'pair'), 0, 0, tiled=True)]
  transfers between devices with their start and end apart: 1 -> 3, of which waited for: 1 -> 2; matrix products, arithmetic and copies ran while one was open for 1% -> 0% of each run, Pallas kernels for 0% -> 0%
where the time goes in v1:
time: 31.6 us; the launch traced here: 31.2 us
  blocking collectives  18 us (57%)
  Pallas kernels  5.83 us (18%)
  waiting for transfers between devices  2.86 us (9%)
  local copies, waits for them, and re-layouts  2.67 us (8%)
  starting transfers between devices  1.86 us (6%)
    all_to_all x1, blocking collectives, exchanged_shards(): turned = lax.all_to_all(sent, ('chan', 'pair'), 0, 0, tiled=True)  18 us
    ppermute x3, waiting for transfers between devices, exchanged_shards(): lax.ppermute(pieces[j], 'pair', [(i, i ^ j) for i in range(blocks)])  2.86 us
    pallas_call x1, Pallas kernels, exchanged_shards(): pl.pallas_call(functools.partial(channelize_kernel, antennas, batches, fr...  2.27 us
    pallas_call x1, Pallas kernels, exchanged_shards(): pl.pallas_call(functools.partial(correlate_kernel, groups, blocks, antenn...  1.96 us
    ppermute x3, starting transfers between devices, exchanged_shards(): lax.ppermute(pieces[j], 'pair', [(i, i ^ j) for i in range(blocks)])  1.86 us
    pallas_call x1, Pallas kernels, exchanged_shards(): pl.pallas_call(functools.partial(place_kernel, blocks), out_shape=jax.Sha...  1.61 us
    reshape x1, local copies, waits for them, and re-layouts, exchanged_shards(): lined = voltages.reshape(antennas, batches, frames * parts, LANES)  1.13 us
    transpose x1, local copies, waits for them, and re-layouts, exchanged_shards(): lined = jnp.transpose(lined, (0, 2, 1, 3)).reshape(rows, LANES)  0.92 us
  transfers between devices with their start and end apart: 3, of which 2 were waited for; matrix products, arithmetic and copies ran while one was open for 0% of the time, Pallas kernels for 0%

profile of v1, /device:TPU:0, one launch (start us, length us, event | category | flops | bytes accessed | tf_op | source)
XLA Modules:
  0.0 31.2 jit_solution(4127228692958749210)
XLA Ops:
  0.0 1.1 %reshape.12 = bf16[2,2,270,128]{3,2,1,0:T(8,128)(2,1)S(1)} reshape(bf16[1,2,2,34560]{3,2,1,0:T(2,128)(2,1)} %param.3) | data formatting | bytes 552960 | tf_op jit(solution)/shard_map/reshape | solution.py:157
  1.1 0.9 %copy.5 = bf16[2,270,2,128]{3,2,1,0:T(2,128)(2,1)} copy(bf16[2,270,2,128]{3,1,2,0:T(8,128)(2,1)S(1)} %bitcast.4) | data formatting | bytes 552960 | tf_op jit(solution)/shard_map/transpose | solution.py:158
  2.1 2.3 %channelize.1 = bf16[32,2,8,256]{3,2,1,0:T(8,128)(2,1)} custom-call(bf16[1080,128]{1,0:T(8,128)(2,1)} %bitcast.5, f32[8,256]{1,0:T(8,128)} %taps_ref.1, bf16[256,256]{1,0:T(8,128)(2,1)} %constant.2.clone.dft_ref), custom_call_target="tpu_custom_call" | custom-call | tf_op jit(solution)/shard_map/channelize/pallas_call | solution.py:161
  4.3 18.0 %all_to_all.5 = bf16[32,16,256]{2,1,0:T(8,128)(2,1)} all-to-all(bf16[32,16,256]{2,1,0:T(8,128)(2,1)} %bitcast.7), channel_id=1, replica_groups=mesh['chan'=8,'pair'=4] {'chan','pair'}, dimensions={0} | all-to-all | bytes 524288 | tf_op jit(solution)/shard_map/all_to_all | solution.py:175
  22.3 2.0 %correlate.1 = (f32[4,16,128]{2,1,0:T(8,128)}, f32[4,16,128]{2,1,0:T(8,128)}, f32[4,16,128]{2,1,0:T(8,128)}, f32[4,16,128]{2,1,0:T(8,128)}) custom-call(bf16[512,256]{1,0:T(8,128)(2,1)} %bitcast.6), custom_call_target="tpu_custom_call" | custom-call | tf_op jit(solution)/shard_map/correlate/pallas_call | solution.py:177
  24.3 0.0 collective-permute-start
  24.3 0.8 %collective-permute-start.1 = (f32[4,16,128]{2,1,0:T(8,128)}, f32[4,16,128]{2,1,0:T(8,128)S(1)}, u32[]{:S(2)}, u32[]{:S(2)}) collective-permute-start(f32[4,16,128]{2,1,0:T(8,128)} %get-tuple-element.11), channel_id=1, source_target_pairs={{0,2},{1,3},{2,0},{3,1},{4,6},{5,7},{6,4},{7,5},{8,10},{9,11},{10,... | collective-permute-start | bytes 98312 | tf_op jit(solution)/shard_map/ppermute | solution.py:198
  25.1 1.0 %collective-permute-start.2 = (f32[4,16,128]{2,1,0:T(8,128)}, f32[4,16,128]{2,1,0:T(8,128)S(1)}, u32[]{:S(2)}, u32[]{:S(2)}) collective-permute-start(f32[4,16,128]{2,1,0:T(8,128)} %get-tuple-element.12), channel_id=1, source_target_pairs={{0,3},{1,2},{2,1},{3,0},{4,7},{5,6},{6,5},{7,4},{8,11},{9,10},{10,... | collective-permute-start | bytes 98312 | tf_op jit(solution)/shard_map/ppermute | solution.py:198
  26.1 0.0 collective-permute-done.refs_1_
  26.1 0.0 copy-start
  26.1 2.4 %collective-permute-done.1.refs_2_ = f32[4,16,128]{2,1,0:T(8,128)S(1)} collective-permute-done((f32[4,16,128]{2,1,0:T(8,128)}, f32[4,16,128]{2,1,0:T(8,128)S(1)}, u32[]{:S(2)}, u32[]{:S(2)}) %collective-permute-start.1) | collective-permute-done | bytes 32800 | tf_op jit(solution)/shard_map/ppermute | solution.py:198
  28.5 0.0 copy-start.1
  28.5 0.5 %collective-permute-done.2.refs_3_ = f32[4,16,128]{2,1,0:T(8,128)S(1)} collective-permute-done((f32[4,16,128]{2,1,0:T(8,128)}, f32[4,16,128]{2,1,0:T(8,128)S(1)}, u32[]{:S(2)}, u32[]{:S(2)}) %collective-permute-start.2) | collective-permute-done | bytes 32800 | tf_op jit(solution)/shard_map/ppermute | solution.py:198
  29.0 0.0 copy-start.2
  29.0 0.0 copy-done
  29.0 0.1 copy-done.1
  29.1 0.5 %copy-done.2 = f32[4,16,128]{2,1,0:T(8,128)} copy-done((f32[4,16,128]{2,1,0:T(8,128)}, f32[4,16,128]{2,1,0:T(8,128)S(1)}, u32[]{:S(2)}) %copy-start.2) | copy-done | bytes 32792
  29.6 1.6 %place.1 = f32[16,2,16,64]{3,2,1,0:T(8,128)} custom-call(f32[4,16,128]{2,1,0:T(8,128)} %get-tuple-element.9.refs_0_, f32[4,16,128]{2,1,0:T(8,128)} %copy-done, f32[4,16,128]{2,1,0:T(8,128)} %copy-done.1, f32[4,16,128]{2,1,0:T(8,128)} %copy-done.2), custom_call_target="tpu_custom_call" | custom-call | tf_op jit(solution)/shard_map/place/pallas_call | solution.py:201
Async XLA Ops:
  24.3 1.9 %collective-permute-start = (f32[4,16,128]{2,1,0:T(8,128)}, f32[4,16,128]{2,1,0:T(8,128)S(1)}, u32[]{:S(2)}, u32[]{:S(2)}) collective-permute-start(f32[4,16,128]{2,1,0:T(8,128)} %get-tuple-element.10), channel_id=1, source_target_pairs={{0,1},{1,0},{2,3},{3,2},{4,5},{5,4},{6,7},{7,6},{8,9},{9,8},{10,11... | collective-permute-start | bytes 98312 | tf_op jit(solution)/shard_map/ppermute | solution.py:198
  24.3 4.2 %collective-permute-start.1 = (f32[4,16,128]{2,1,0:T(8,128)}, f32[4,16,128]{2,1,0:T(8,128)S(1)}, u32[]{:S(2)}, u32[]{:S(2)}) collective-permute-start(f32[4,16,128]{2,1,0:T(8,128)} %get-tuple-element.11), channel_id=1, source_target_pairs={{0,2},{1,3},{2,0},{3,1},{4,6},{5,7},{6,4},{7,5},{8,10},{9,11},{10,... | collective-permute-start | bytes 98312 | tf_op jit(solution)/shard_map/ppermute | solution.py:198
  25.1 3.9 %collective-permute-start.2 = (f32[4,16,128]{2,1,0:T(8,128)}, f32[4,16,128]{2,1,0:T(8,128)S(1)}, u32[]{:S(2)}, u32[]{:S(2)}) collective-permute-start(f32[4,16,128]{2,1,0:T(8,128)} %get-tuple-element.12), channel_id=1, source_target_pairs={{0,3},{1,2},{2,1},{3,0},{4,7},{5,6},{6,5},{7,4},{8,11},{9,10},{10,... | collective-permute-start | bytes 98312 | tf_op jit(solution)/shard_map/ppermute | solution.py:198
  26.1 2.9 %copy-start = (f32[4,16,128]{2,1,0:T(8,128)}, f32[4,16,128]{2,1,0:T(8,128)S(1)}, u32[]{:S(2)}) copy-start(f32[4,16,128]{2,1,0:T(8,128)S(1)} %collective-permute-done.refs_1_) | copy-start | bytes 98308
  28.5 0.6 %copy-start.1 = (f32[4,16,128]{2,1,0:T(8,128)}, f32[4,16,128]{2,1,0:T(8,128)S(1)}, u32[]{:S(2)}) copy-start(f32[4,16,128]{2,1,0:T(8,128)S(1)} %collective-permute-done.1.refs_2_) | copy-start | bytes 98308
  29.0 0.6 %copy-start.2 = (f32[4,16,128]{2,1,0:T(8,128)}, f32[4,16,128]{2,1,0:T(8,128)S(1)}, u32[]{:S(2)}) copy-start(f32[4,16,128]{2,1,0:T(8,128)S(1)} %collective-permute-done.2.refs_3_) | copy-start | bytes 98308

commit v2 on v1

--- a/solution.py
+++ b/solution.py
@@ -10,6 +10,7 @@
 from jax.sharding import PartitionSpec as P
 
 LANES = 128
+LIMIT = 16 * 2**20
 VMEM = pltpu.MemorySpace.VMEM
 
 
@@ -169,6 +170,7 @@
             pltpu.VMEM((rows, LANES), jnp.float32),
             pltpu.VMEM((antennas, batches * spectra, frame), jnp.bfloat16),
         ],
+        compiler_params=pltpu.CompilerParams(vmem_limit_bytes=LIMIT),
         name="channelize",
     )(lined, fir_taps, table)
     sent = sent.reshape(devices, antennas * 2 * channels, batches * spectra)
@@ -192,6 +194,7 @@
             ),
             pltpu.VMEM((blocks, channels, total // blocks, 2 * total), jnp.float32),
         ],
+        compiler_params=pltpu.CompilerParams(vmem_limit_bytes=LIMIT),
         name="correlate",
     )(turned.reshape(devices * antennas * 2 * channels, batches * spectra))
     arrived = [pieces[0]] + [
@@ -205,6 +208,7 @@
         ),
         in_specs=[vmem] * blocks,
         out_specs=vmem,
+        compiler_params=pltpu.CompilerParams(vmem_limit_bytes=LIMIT),
         name="place",
     )(*arrived)
 

time: 31.6 us -> 26.2 us (0.83)
  Pallas kernels: 5.83 us -> 1.71 us
  local copies, waits for them, and re-layouts: 2.67 us -> 2.02 us
    pallas_call x1, Pallas kernels: 2.27 us -> 0.55 us  [exchanged_shards(): pl.pallas_call(functools.partial(channelize_kernel, antennas, batches, fr...]
    pallas_call x1, Pallas kernels: 1.96 us -> 0.35 us  [exchanged_shards(): pl.pallas_call(functools.partial(correlate_kernel, groups, blocks, antenn...]
    pallas_call x1, Pallas kernels: 1.61 us -> 0.8 us  [exchanged_shards(): pl.pallas_call(functools.partial(place_kernel, blocks), out_shape=jax.Sha...]
    transpose x1, local copies, waits for them, and re-layouts: 0.92 us -> 0.21 us  [exchanged_shards(): lined = jnp.transpose(lined, (0, 2, 1, 3)).reshape(rows, LANES)]
    unnamed x6 -> x4, local copies, waits for them, and re-layouts: 0.62 us -> 0.67 us
where the time goes in v2:
time: 26.2 us; the launch traced here: 26.1 us
  blocking collectives  17.7 us (68%)
  waiting for transfers between devices  2.65 us (10%)
  local copies, waits for them, and re-layouts  2.02 us (8%)
  starting transfers between devices  1.92 us (7%)
  Pallas kernels  1.71 us (7%)
    all_to_all x1, blocking collectives, exchanged_shards(): turned = lax.all_to_all(sent, ('chan', 'pair'), 0, 0, tiled=True)  17.7 us
    ppermute x3, waiting for transfers between devices, exchanged_shards(): lax.ppermute(pieces[j], 'pair', [(i, i ^ j) for i in range(blocks)])  2.65 us
    ppermute x3, starting transfers between devices, exchanged_shards(): lax.ppermute(pieces[j], 'pair', [(i, i ^ j) for i in range(blocks)])  1.92 us
    reshape x1, local copies, waits for them, and re-layouts, exchanged_shards(): lined = voltages.reshape(antennas, batches, frames * parts, LANES)  1.13 us
    pallas_call x1, Pallas kernels, exchanged_shards(): pl.pallas_call(functools.partial(place_kernel, blocks), out_shape=jax.Sha...  0.8 us
    unnamed x4, local copies, waits for them, and re-layouts  0.67 us
    pallas_call x1, Pallas kernels, exchanged_shards(): pl.pallas_call(functools.partial(channelize_kernel, antennas, batches, fr...  0.55 us
  transfers between devices with their start and end apart: 3, of which 2 were waited for; matrix products, arithmetic and copies ran while one was open for 0% of the time, Pallas kernels for 0%

profile of v2, /device:TPU:0, one launch (start us, length us, event | category | flops | bytes accessed | tf_op | source)
XLA Modules:
  0.0 26.1 jit_solution(13635397683906371765)
XLA Ops:
  0.0 1.1 %reshape.12 = bf16[2,2,270,128]{3,2,1,0:T(8,128)(2,1)S(1)} reshape(bf16[1,2,2,34560]{3,2,1,0:T(2,128)(2,1)} %param.3) | data formatting | bytes 552960 | tf_op jit(solution)/shard_map/reshape | solution.py:158
  1.1 0.0 copy-start
  1.1 0.0 copy-start.1
  1.2 0.2 copy.5
  1.4 0.7 %copy-done = bf16[256,256]{1,0:T(8,128)(2,1)S(1)} copy-done((bf16[256,256]{1,0:T(8,128)(2,1)S(1)}, bf16[256,256]{1,0:T(8,128)(2,1)}, u32[]{:S(2)}) %copy-start) | copy-done | bytes 131096
  2.0 0.0 copy-done.1
  2.0 0.6 %channelize.1 = bf16[32,2,8,256]{3,2,1,0:T(8,128)(2,1)S(1)} custom-call(bf16[1080,128]{1,0:T(8,128)(2,1)S(1)} %bitcast.4, f32[8,256]{1,0:T(8,128)S(1)} %copy-done.1, bf16[256,256]{1,0:T(8,128)(2,1)S(1)} %copy-done), custom_call_target="tpu_custom_call" | custom-call | tf_op jit(solution)/shard_map/channelize/pallas_call | solution.py:162
  2.6 17.7 %all_to_all.5 = bf16[32,16,256]{2,1,0:T(8,128)(2,1)S(1)} all-to-all(bf16[32,16,256]{2,1,0:T(8,128)(2,1)S(1)} %bitcast.6), channel_id=1, replica_groups=mesh['chan'=8,'pair'=4] {'chan','pair'}, dimensions={0} | all-to-all | bytes 524288 | tf_op jit(solution)/shard_map/all_to_all | solution.py:177
  20.3 0.4 %correlate.1 = (f32[4,16,128]{2,1,0:T(8,128)S(1)}, f32[4,16,128]{2,1,0:T(8,128)S(1)}, f32[4,16,128]{2,1,0:T(8,128)S(1)}, f32[4,16,128]{2,1,0:T(8,128)S(1)}) custom-call(bf16[512,256]{1,0:T(8,128)(2,1)S(1)} %bitcast.5), custom_call_target="tpu_custom_call" | custom-call | tf_op jit(solution)/shard_map/correlate/pallas_call | solution.py:179
  20.7 0.1 collective-permute-start
  20.8 0.8 %collective-permute-start.1 = (f32[4,16,128]{2,1,0:T(8,128)S(1)}, f32[4,16,128]{2,1,0:T(8,128)S(1)}, u32[]{:S(2)}, u32[]{:S(2)}) collective-permute-start(f32[4,16,128]{2,1,0:T(8,128)S(1)} %get-tuple-element.11), channel_id=1, source_target_pairs={{0,2},{1,3},{2,0},{3,1},{4,6},{5,7},{6,4},{7,5},{8,10},{9,11},{10,... | collective-permute-start | bytes 98312 | tf_op jit(solution)/shard_map/ppermute | solution.py:201
  21.6 1.0 %collective-permute-start.2 = (f32[4,16,128]{2,1,0:T(8,128)S(1)}, f32[4,16,128]{2,1,0:T(8,128)S(1)}, u32[]{:S(2)}, u32[]{:S(2)}) collective-permute-start(f32[4,16,128]{2,1,0:T(8,128)S(1)} %get-tuple-element.12), channel_id=1, source_target_pairs={{0,3},{1,2},{2,1},{3,0},{4,7},{5,6},{6,5},{7,4},{8,11},{9,10},{10,... | collective-permute-start | bytes 98312 | tf_op jit(solution)/shard_map/ppermute | solution.py:201
  22.6 0.0 collective-permute-done.refs_1_
  22.6 2.3 %collective-permute-done.1.refs_2_ = f32[4,16,128]{2,1,0:T(8,128)S(1)} collective-permute-done((f32[4,16,128]{2,1,0:T(8,128)S(1)}, f32[4,16,128]{2,1,0:T(8,128)S(1)}, u32[]{:S(2)}, u32[]{:S(2)}) %collective-permute-start.1) | collective-permute-done | bytes 32800 | tf_op jit(solution)/shard_map/ppermute | solution.py:201
  24.9 0.3 %collective-permute-done.2.refs_3_ = f32[4,16,128]{2,1,0:T(8,128)S(1)} collective-permute-done((f32[4,16,128]{2,1,0:T(8,128)S(1)}, f32[4,16,128]{2,1,0:T(8,128)S(1)}, u32[]{:S(2)}, u32[]{:S(2)}) %collective-permute-start.2) | collective-permute-done | bytes 32800 | tf_op jit(solution)/shard_map/ppermute | solution.py:201
  25.3 0.8 %place.1 = f32[16,2,16,64]{3,2,1,0:T(8,128)} custom-call(f32[4,16,128]{2,1,0:T(8,128)S(1)} %get-tuple-element.9.refs_0_, f32[4,16,128]{2,1,0:T(8,128)S(1)} %collective-permute-done.refs_1_, f32[4,16,128]{2,1,0:T(8,128)S(1)} %collective-permute-done.1.refs_2_, f32[4,16,128]{2,1,0:T(8,128)S(1)} %collective-permute-done.2.refs_3_), custom_call_target="tpu_custom_call" | custom-call | tf_op jit(solution)/shard_map/place/pallas_call | solution.py:204
Async XLA Ops:
  1.1 0.9 %copy-start = (bf16[256,256]{1,0:T(8,128)(2,1)S(1)}, bf16[256,256]{1,0:T(8,128)(2,1)}, u32[]{:S(2)}) copy-start(bf16[256,256]{1,0:T(8,128)(2,1)} %constant.2.clone.dft_ref) | copy-start | bytes 393220
  1.1 0.9 %copy-start.1 = (f32[8,256]{1,0:T(8,128)S(1)}, f32[8,256]{1,0:T(8,128)}, u32[]{:S(2)}) copy-start(f32[8,256]{1,0:T(8,128)} %taps_ref.1) | copy-start | bytes 24580
  20.7 1.9 %collective-permute-start = (f32[4,16,128]{2,1,0:T(8,128)S(1)}, f32[4,16,128]{2,1,0:T(8,128)S(1)}, u32[]{:S(2)}, u32[]{:S(2)}) collective-permute-start(f32[4,16,128]{2,1,0:T(8,128)S(1)} %get-tuple-element.10), channel_id=1, source_target_pairs={{0,1},{1,0},{2,3},{3,2},{4,5},{5,4},{6,7},{7,6},{8,9},{9,8},{10,11... | collective-permute-start | bytes 98312 | tf_op jit(solution)/shard_map/ppermute | solution.py:201
  20.8 4.2 %collective-permute-start.1 = (f32[4,16,128]{2,1,0:T(8,128)S(1)}, f32[4,16,128]{2,1,0:T(8,128)S(1)}, u32[]{:S(2)}, u32[]{:S(2)}) collective-permute-start(f32[4,16,128]{2,1,0:T(8,128)S(1)} %get-tuple-element.11), channel_id=1, source_target_pairs={{0,2},{1,3},{2,0},{3,1},{4,6},{5,7},{6,4},{7,5},{8,10},{9,11},{10,... | collective-permute-start | bytes 98312 | tf_op jit(solution)/shard_map/ppermute | solution.py:201
  21.6 3.7 %collective-permute-start.2 = (f32[4,16,128]{2,1,0:T(8,128)S(1)}, f32[4,16,128]{2,1,0:T(8,128)S(1)}, u32[]{:S(2)}, u32[]{:S(2)}) collective-permute-start(f32[4,16,128]{2,1,0:T(8,128)S(1)} %get-tuple-element.12), channel_id=1, source_target_pairs={{0,3},{1,2},{2,1},{3,0},{4,7},{5,6},{6,5},{7,4},{8,11},{9,10},{10,... | collective-permute-start | bytes 98312 | tf_op jit(solution)/shard_map/ppermute | solution.py:201

commit v3 on v2

--- a/solution.py
+++ b/solution.py
@@ -81,22 +81,33 @@
     return summed * (1.0 / math.sqrt(batch_count * spectra_len))
 
 
-def channelize_kernel(antennas, batches, frames, v_ref, taps_ref, dft_ref, o_ref, x_ref, f_ref):
+def channelize_kernel(v_hbm, taps_hbm, dft_hbm, o_ref, v_ref, taps_ref, dft_ref, x_ref, f_ref, sems):
+    antennas, batches, length = v_ref.shape
     taps, frame = taps_ref.shape
+    copies = [pltpu.make_async_copy(v_hbm.at[a], v_ref.at[a], sems.at[a]) for a in range(antennas)]
+    copy_taps = pltpu.make_async_copy(taps_hbm, taps_ref, sems.at[antennas])
+    copy_dft = pltpu.make_async_copy(dft_hbm, dft_ref, sems.at[antennas + 1])
+    for copy in [copy_taps] + copies + [copy_dft]:
+        copy.start()
+    copy_taps.wait()
     parts = frame // LANES
-    step = parts * batches
-    spectra = frames - taps + 1
-    x_ref[...] = v_ref[...].astype(jnp.float32)
+    spectra = length // frame - taps + 1
     for a in range(antennas):
+        copies[a].wait()
+        samples = v_ref[a].astype(jnp.float32)
+        for b in range(batches):
+            x_ref[a, b] = samples[b].reshape(length // LANES, LANES)
         for b in range(batches):
             for h in range(parts):
                 lanes = slice(h * LANES, (h + 1) * LANES)
                 total = None
                 for p in range(taps):
-                    first = (a * frames + p) * step + h * batches + b
-                    term = taps_ref[p : p + 1, lanes] * x_ref[pl.ds(first, spectra, stride=step), :]
+                    rows = x_ref[a, b, pl.ds(p * parts + h, spectra, stride=parts), :]
+                    term = taps_ref[p : p + 1, lanes] * rows
                     total = term if total is None else total + term
                 f_ref[a, b * spectra : (b + 1) * spectra, lanes] = total.astype(jnp.bfloat16)
+        if a == 0:
+            copy_dft.wait()
         spec = lax.dot_general(
             dft_ref[...], f_ref[a], (((1,), (1,)), ((), ())), preferred_element_type=jnp.float32
         )
@@ -150,29 +161,30 @@
     taps, frame = fir_taps.shape
     frames = length // frame
     spectra = frames - taps + 1
-    parts = frame // LANES
     devices = groups * blocks
     channels = frame // 2 // devices
     total = devices * antennas
-    rows = antennas * frames * parts * batches
-    lined = voltages.reshape(antennas, batches, frames * parts, LANES)
-    lined = jnp.transpose(lined, (0, 2, 1, 3)).reshape(rows, LANES)
     table = jnp.asarray(dft_table(frame // 2), jnp.bfloat16)
     vmem = pl.BlockSpec(memory_space=VMEM)
+    hbm = pl.BlockSpec(memory_space=pltpu.MemorySpace.HBM)
     sent = pl.pallas_call(
-        functools.partial(channelize_kernel, antennas, batches, frames),
+        channelize_kernel,
         out_shape=jax.ShapeDtypeStruct(
             (devices, antennas, 2 * channels, batches * spectra), jnp.bfloat16
         ),
-        in_specs=[vmem] * 3,
+        in_specs=[hbm] * 3,
         out_specs=vmem,
         scratch_shapes=[
-            pltpu.VMEM((rows, LANES), jnp.float32),
+            pltpu.VMEM((antennas, batches, length), jnp.bfloat16),
+            pltpu.VMEM((taps, frame), jnp.float32),
+            pltpu.VMEM((frame, frame), jnp.bfloat16),
+            pltpu.VMEM((antennas, batches, length // LANES, LANES), jnp.float32),
             pltpu.VMEM((antennas, batches * spectra, frame), jnp.bfloat16),
+            pltpu.SemaphoreType.DMA((antennas + 2,)),
         ],
         compiler_params=pltpu.CompilerParams(vmem_limit_bytes=LIMIT),
         name="channelize",
-    )(lined, fir_taps, table)
+    )(*[pltpu.with_memory_space_constraint(x, pltpu.MemorySpace.HBM) for x in (voltages[0], fir_taps, table)])
     sent = sent.reshape(devices, antennas * 2 * channels, batches * spectra)
     turned = lax.all_to_all(sent, ("chan", "pair"), 0, 0, tiled=True)
     own_shape = jax.ShapeDtypeStruct((channels, total // blocks, 2 * total), jnp.float32)

time: 26.2 us -> 25.5 us (0.973)
  local copies, waits for them, and re-layouts: 2.02 us -> 0 us
  Pallas kernels: 1.71 us -> 2.96 us
    pallas_call x1, Pallas kernels: 0.55 us -> 1.8 us  [exchanged_shards(): pl.pallas_call(channelize_kernel, out_shape=jax.ShapeDtypeStruct((devices...]
    reshape x1 -> x0, local copies, waits for them, and re-layouts: 1.13 us -> none  [exchanged_shards(): lined = voltages.reshape(antennas, batches, frames * parts, LANES)]
    unnamed x4 -> x0, local copies, waits for them, and re-layouts: 0.67 us -> none
where the time goes in v3:
time: 25.5 us; the launch traced here: 25.3 us
  blocking collectives  17.7 us (69%)
  Pallas kernels  2.96 us (12%)
  waiting for transfers between devices  2.65 us (10%)
  starting transfers between devices  1.92 us (8%)
    all_to_all x1, blocking collectives, exchanged_shards(): turned = lax.all_to_all(sent, ('chan', 'pair'), 0, 0, tiled=True)  17.7 us
    ppermute x3, waiting for transfers between devices, exchanged_shards(): lax.ppermute(pieces[j], 'pair', [(i, i ^ j) for i in range(blocks)])  2.65 us
    ppermute x3, starting transfers between devices, exchanged_shards(): lax.ppermute(pieces[j], 'pair', [(i, i ^ j) for i in range(blocks)])  1.92 us
    pallas_call x1, Pallas kernels, exchanged_shards(): pl.pallas_call(channelize_kernel, out_shape=jax.ShapeDtypeStruct((devices...  1.8 us
    pallas_call x1, Pallas kernels, exchanged_shards(): pl.pallas_call(functools.partial(place_kernel, blocks), out_shape=jax.Sha...  0.8 us
  transfers between devices with their start and end apart: 3, of which 2 were waited for; matrix products, arithmetic and copies ran while one was open for 0% of the time, Pallas kernels for 0%

profile of v3, /device:TPU:0, one launch (start us, length us, event | category | flops | bytes accessed | tf_op | source)
XLA Modules:
  0.0 25.3 jit_solution(609905358758681345)
XLA Ops:
  0.0 1.8 %channelize.1 = bf16[32,2,8,256]{3,2,1,0:T(8,128)(2,1)S(1)} custom-call(bf16[2,2,34560]{2,1,0:T(2,128)(2,1)} %bitcast.5, f32[8,256]{1,0:T(8,128)} %taps_hbm.1, bf16[256,256]{1,0:T(8,128)(2,1)} %constant.2.clone.dft_hbm), custom_call_target="tpu_custom_call" | custom-call | tf_op jit(solution)/shard_map/channelize/pallas_call | solution.py:170
  1.8 17.7 %all_to_all.5 = bf16[32,16,256]{2,1,0:T(8,128)(2,1)S(1)} all-to-all(bf16[32,16,256]{2,1,0:T(8,128)(2,1)S(1)} %bitcast.4), channel_id=1, replica_groups=mesh['chan'=8,'pair'=4] {'chan','pair'}, dimensions={0} | all-to-all | bytes 524288 | tf_op jit(solution)/shard_map/all_to_all | solution.py:189
  19.5 0.4 %correlate.1 = (f32[4,16,128]{2,1,0:T(8,128)S(1)}, f32[4,16,128]{2,1,0:T(8,128)S(1)}, f32[4,16,128]{2,1,0:T(8,128)S(1)}, f32[4,16,128]{2,1,0:T(8,128)S(1)}) custom-call(bf16[512,256]{1,0:T(8,128)(2,1)S(1)} %bitcast.3), custom_call_target="tpu_custom_call" | custom-call | tf_op jit(solution)/shard_map/correlate/pallas_call | solution.py:191
  19.9 0.1 collective-permute-start
  20.0 0.8 %collective-permute-start.1 = (f32[4,16,128]{2,1,0:T(8,128)S(1)}, f32[4,16,128]{2,1,0:T(8,128)S(1)}, u32[]{:S(2)}, u32[]{:S(2)}) collective-permute-start(f32[4,16,128]{2,1,0:T(8,128)S(1)} %get-tuple-element.11), channel_id=1, source_target_pairs={{0,2},{1,3},{2,0},{3,1},{4,6},{5,7},{6,4},{7,5},{8,10},{9,11},{10,... | collective-permute-start | bytes 98312 | tf_op jit(solution)/shard_map/ppermute | solution.py:213
  20.8 1.0 %collective-permute-start.2 = (f32[4,16,128]{2,1,0:T(8,128)S(1)}, f32[4,16,128]{2,1,0:T(8,128)S(1)}, u32[]{:S(2)}, u32[]{:S(2)}) collective-permute-start(f32[4,16,128]{2,1,0:T(8,128)S(1)} %get-tuple-element.12), channel_id=1, source_target_pairs={{0,3},{1,2},{2,1},{3,0},{4,7},{5,6},{6,5},{7,4},{8,11},{9,10},{10,... | collective-permute-start | bytes 98312 | tf_op jit(solution)/shard_map/ppermute | solution.py:213
  21.8 0.0 collective-permute-done.refs_1_
  21.8 2.3 %collective-permute-done.1.refs_2_ = f32[4,16,128]{2,1,0:T(8,128)S(1)} collective-permute-done((f32[4,16,128]{2,1,0:T(8,128)S(1)}, f32[4,16,128]{2,1,0:T(8,128)S(1)}, u32[]{:S(2)}, u32[]{:S(2)}) %collective-permute-start.1) | collective-permute-done | bytes 32800 | tf_op jit(solution)/shard_map/ppermute | solution.py:213
  24.1 0.3 %collective-permute-done.2.refs_3_ = f32[4,16,128]{2,1,0:T(8,128)S(1)} collective-permute-done((f32[4,16,128]{2,1,0:T(8,128)S(1)}, f32[4,16,128]{2,1,0:T(8,128)S(1)}, u32[]{:S(2)}, u32[]{:S(2)}) %collective-permute-start.2) | collective-permute-done | bytes 32800 | tf_op jit(solution)/shard_map/ppermute | solution.py:213
  24.5 0.8 %place.1 = f32[16,2,16,64]{3,2,1,0:T(8,128)} custom-call(f32[4,16,128]{2,1,0:T(8,128)S(1)} %get-tuple-element.9.refs_0_, f32[4,16,128]{2,1,0:T(8,128)S(1)} %collective-permute-done.refs_1_, f32[4,16,128]{2,1,0:T(8,128)S(1)} %collective-permute-done.1.refs_2_, f32[4,16,128]{2,1,0:T(8,128)S(1)} %collective-permute-done.2.refs_3_), custom_call_target="tpu_custom_call" | custom-call | tf_op jit(solution)/shard_map/place/pallas_call | solution.py:216
Async XLA Ops:
  19.9 1.9 %collective-permute-start = (f32[4,16,128]{2,1,0:T(8,128)S(1)}, f32[4,16,128]{2,1,0:T(8,128)S(1)}, u32[]{:S(2)}, u32[]{:S(2)}) collective-permute-start(f32[4,16,128]{2,1,0:T(8,128)S(1)} %get-tuple-element.10), channel_id=1, source_target_pairs={{0,1},{1,0},{2,3},{3,2},{4,5},{5,4},{6,7},{7,6},{8,9},{9,8},{10,11... | collective-permute-start | bytes 98312 | tf_op jit(solution)/shard_map/ppermute | solution.py:213
  20.0 4.2 %collective-permute-start.1 = (f32[4,16,128]{2,1,0:T(8,128)S(1)}, f32[4,16,128]{2,1,0:T(8,128)S(1)}, u32[]{:S(2)}, u32[]{:S(2)}) collective-permute-start(f32[4,16,128]{2,1,0:T(8,128)S(1)} %get-tuple-element.11), channel_id=1, source_target_pairs={{0,2},{1,3},{2,0},{3,1},{4,6},{5,7},{6,4},{7,5},{8,10},{9,11},{10,... | collective-permute-start | bytes 98312 | tf_op jit(solution)/shard_map/ppermute | solution.py:213
  20.8 3.7 %collective-permute-start.2 = (f32[4,16,128]{2,1,0:T(8,128)S(1)}, f32[4,16,128]{2,1,0:T(8,128)S(1)}, u32[]{:S(2)}, u32[]{:S(2)}) collective-permute-start(f32[4,16,128]{2,1,0:T(8,128)S(1)} %get-tuple-element.12), channel_id=1, source_target_pairs={{0,3},{1,2},{2,1},{3,0},{4,7},{5,6},{6,5},{7,4},{8,11},{9,10},{10,... | collective-permute-start | bytes 98312 | tf_op jit(solution)/shard_map/ppermute | solution.py:213

commit v4 on v3

--- a/solution.py
+++ b/solution.py
@@ -87,7 +87,7 @@
     copies = [pltpu.make_async_copy(v_hbm.at[a], v_ref.at[a], sems.at[a]) for a in range(antennas)]
     copy_taps = pltpu.make_async_copy(taps_hbm, taps_ref, sems.at[antennas])
     copy_dft = pltpu.make_async_copy(dft_hbm, dft_ref, sems.at[antennas + 1])
-    for copy in [copy_taps] + copies + [copy_dft]:
+    for copy in copies + [copy_taps, copy_dft]:
         copy.start()
     copy_taps.wait()
     parts = frame // LANES
@@ -106,8 +106,8 @@
                     term = taps_ref[p : p + 1, lanes] * rows
                     total = term if total is None else total + term
                 f_ref[a, b * spectra : (b + 1) * spectra, lanes] = total.astype(jnp.bfloat16)
-        if a == 0:
-            copy_dft.wait()
+    copy_dft.wait()
+    for a in range(antennas):
         spec = lax.dot_general(
             dft_ref[...], f_ref[a], (((1,), (1,)), ((), ())), preferred_element_type=jnp.float32
         )
@@ -141,7 +141,7 @@
         vis[:, c, :, :] = (prod * scale).reshape(blocks, total // blocks, 2 * total)
     me = lax.axis_index("pair")
     for j in range(blocks):
-        outs[j][...] = vis[me ^ j]
+        outs[j][...] = vis[me ^ j].astype(outs[j].dtype)
 
 
 def place_kernel(blocks, *refs):
@@ -151,7 +151,7 @@
     me = lax.axis_index("pair")
     for j in range(blocks):
         at = pl.ds((me ^ j) * channels, channels)
-        block = ins[j][...]
+        block = ins[j][...].astype(jnp.float32)
         o_ref[at, 0, :, :] = block[:, :, :columns]
         o_ref[at, 1, :, :] = block[:, :, columns:]
 
@@ -187,7 +187,8 @@
     )(*[pltpu.with_memory_space_constraint(x, pltpu.MemorySpace.HBM) for x in (voltages[0], fir_taps, table)])
     sent = sent.reshape(devices, antennas * 2 * channels, batches * spectra)
     turned = lax.all_to_all(sent, ("chan", "pair"), 0, 0, tiled=True)
-    own_shape = jax.ShapeDtypeStruct((channels, total // blocks, 2 * total), jnp.float32)
+    piece = (channels, total // blocks, 2 * total)
+    kinds = [jnp.float32 if j < 2 else jnp.bfloat16 for j in range(blocks)]
     pieces = pl.pallas_call(
         functools.partial(
             correlate_kernel,
@@ -197,7 +198,7 @@
             channels,
             1.0 / math.sqrt(batches * spectra),
         ),
-        out_shape=[own_shape] * blocks,
+        out_shape=[jax.ShapeDtypeStruct(piece, kind) for kind in kinds],
         in_specs=[vmem],
         out_specs=[vmem] * blocks,
         scratch_shapes=[

time: 25.5 us -> 24.8 us (0.973)
  waiting for transfers between devices: 2.65 us -> 2.3 us
    ppermute x3, waiting for transfers between devices: 2.65 us -> 2.3 us  [exchanged_shards(): lax.ppermute(pieces[j], 'pair', [(i, i ^ j) for i in range(blocks)])]
where the time goes in v4:
time: 24.8 us; the launch traced here: 24.7 us
  blocking collectives  17.7 us (71%)
  Pallas kernels  2.72 us (11%)
  waiting for transfers between devices  2.3 us (9%)
  starting transfers between devices  1.92 us (8%)
    all_to_all x1, blocking collectives, exchanged_shards(): turned = lax.all_to_all(sent, ('chan', 'pair'), 0, 0, tiled=True)  17.7 us
    ppermute x3, waiting for transfers between devices, exchanged_shards(): lax.ppermute(pieces[j], 'pair', [(i, i ^ j) for i in range(blocks)])  2.3 us
    ppermute x3, starting transfers between devices, exchanged_shards(): lax.ppermute(pieces[j], 'pair', [(i, i ^ j) for i in range(blocks)])  1.92 us
    pallas_call x1, Pallas kernels, exchanged_shards(): pl.pallas_call(channelize_kernel, out_shape=jax.ShapeDtypeStruct((devices...  1.57 us
    pallas_call x1, Pallas kernels, exchanged_shards(): pl.pallas_call(functools.partial(place_kernel, blocks), out_shape=jax.Sha...  0.8 us
  transfers between devices with their start and end apart: 3, of which 2 were waited for; matrix products, arithmetic and copies ran while one was open for 0% of the time, Pallas kernels for 0%

profile of v4, /device:TPU:0, one launch (start us, length us, event | category | flops | bytes accessed | tf_op | source)
XLA Modules:
  0.0 24.7 jit_solution(3162311496245437229)
XLA Ops:
  0.0 1.6 %channelize.1 = bf16[32,2,8,256]{3,2,1,0:T(8,128)(2,1)S(1)} custom-call(bf16[2,2,34560]{2,1,0:T(2,128)(2,1)} %bitcast.5, f32[8,256]{1,0:T(8,128)} %taps_hbm.1, bf16[256,256]{1,0:T(8,128)(2,1)} %constant.2.clone.dft_hbm), custom_call_target="tpu_custom_call" | custom-call | tf_op jit(solution)/shard_map/channelize/pallas_call | solution.py:170
  1.6 17.7 %all_to_all.5 = bf16[32,16,256]{2,1,0:T(8,128)(2,1)S(1)} all-to-all(bf16[32,16,256]{2,1,0:T(8,128)(2,1)S(1)} %bitcast.4), channel_id=1, replica_groups=mesh['chan'=8,'pair'=4] {'chan','pair'}, dimensions={0} | all-to-all | bytes 524288 | tf_op jit(solution)/shard_map/all_to_all | solution.py:189
  19.3 0.4 %correlate.1 = (f32[4,16,128]{2,1,0:T(8,128)S(1)}, f32[4,16,128]{2,1,0:T(8,128)S(1)}, bf16[4,16,128]{2,1,0:T(8,128)(2,1)S(1)}, bf16[4,16,128]{2,1,0:T(8,128)(2,1)S(1)}) custom-call(bf16[512,256]{1,0:T(8,128)(2,1)S(1)} %bitcast.3), custom_call_target="tpu_custom_call" | custom-call | tf_op jit(solution)/shard_map/correlate/pallas_call | solution.py:192
  19.6 0.1 collective-permute-start
  19.7 0.8 %collective-permute-start.1 = (bf16[4,16,128]{2,1,0:T(8,128)(2,1)S(1)}, bf16[4,16,128]{2,1,0:T(8,128)(2,1)S(1)}, u32[]{:S(2)}, u32[]{:S(2)}) collective-permute-start(bf16[4,16,128]{2,1,0:T(8,128)(2,1)S(1)} %get-tuple-element.11), channel_id=1, source_target_pairs={{0,2},{1,3},{2,0},{3,1},{4,6},{5,7},{6,4},{7,5},{8,10},{9,11},{10,... | collective-permute-start | bytes 49160 | tf_op jit(solution)/shard_map/ppermute | solution.py:214
  20.5 1.0 %collective-permute-start.2 = (bf16[4,16,128]{2,1,0:T(8,128)(2,1)S(1)}, bf16[4,16,128]{2,1,0:T(8,128)(2,1)S(1)}, u32[]{:S(2)}, u32[]{:S(2)}) collective-permute-start(bf16[4,16,128]{2,1,0:T(8,128)(2,1)S(1)} %get-tuple-element.12), channel_id=1, source_target_pairs={{0,3},{1,2},{2,1},{3,0},{4,7},{5,6},{6,5},{7,4},{8,11},{9,10},{10,... | collective-permute-start | bytes 49160 | tf_op jit(solution)/shard_map/ppermute | solution.py:214
  21.6 2.0 %collective-permute-done.1.refs_2_ = bf16[4,16,128]{2,1,0:T(8,128)(2,1)S(1)} collective-permute-done((bf16[4,16,128]{2,1,0:T(8,128)(2,1)S(1)}, bf16[4,16,128]{2,1,0:T(8,128)(2,1)S(1)}, u32[]{:S(2)}, u32[]{:S(2)}) %collective-permute-start.1) | collective-permute-done | bytes 16416 | tf_op jit(solution)/shard_map/ppermute | solution.py:214
  23.5 0.3 %collective-permute-done.2.refs_3_ = bf16[4,16,128]{2,1,0:T(8,128)(2,1)S(1)} collective-permute-done((bf16[4,16,128]{2,1,0:T(8,128)(2,1)S(1)}, bf16[4,16,128]{2,1,0:T(8,128)(2,1)S(1)}, u32[]{:S(2)}, u32[]{:S(2)}) %collective-permute-start.2) | collective-permute-done | bytes 16416 | tf_op jit(solution)/shard_map/ppermute | solution.py:214
  23.9 0.0 collective-permute-done.refs_1_
  23.9 0.8 %place.1 = f32[16,2,16,64]{3,2,1,0:T(8,128)} custom-call(f32[4,16,128]{2,1,0:T(8,128)S(1)} %get-tuple-element.9.refs_0_, f32[4,16,128]{2,1,0:T(8,128)S(1)} %collective-permute-done.refs_1_, bf16[4,16,128]{2,1,0:T(8,128)(2,1)S(1)} %collective-permute-done.1.refs_2_, bf16[4,16,128]{2,1,0:T(8,128)(2,1)S(1)} %collective-permute-done.2.refs_3_), custom_call_target="tpu_custom_call" | custom-call | tf_op jit(solution)/shard_map/place/pallas_call | solution.py:217
Async XLA Ops:
  19.6 4.2 %collective-permute-start = (f32[4,16,128]{2,1,0:T(8,128)S(1)}, f32[4,16,128]{2,1,0:T(8,128)S(1)}, u32[]{:S(2)}, u32[]{:S(2)}) collective-permute-start(f32[4,16,128]{2,1,0:T(8,128)S(1)} %get-tuple-element.10), channel_id=1, source_target_pairs={{0,1},{1,0},{2,3},{3,2},{4,5},{5,4},{6,7},{7,6},{8,9},{9,8},{10,11... | collective-permute-start | bytes 98312 | tf_op jit(solution)/shard_map/ppermute | solution.py:214
  19.7 3.8 %collective-permute-start.1 = (bf16[4,16,128]{2,1,0:T(8,128)(2,1)S(1)}, bf16[4,16,128]{2,1,0:T(8,128)(2,1)S(1)}, u32[]{:S(2)}, u32[]{:S(2)}) collective-permute-start(bf16[4,16,128]{2,1,0:T(8,128)(2,1)S(1)} %get-tuple-element.11), channel_id=1, source_target_pairs={{0,2},{1,3},{2,0},{3,1},{4,6},{5,7},{6,4},{7,5},{8,10},{9,11},{10,... | collective-permute-start | bytes 49160 | tf_op jit(solution)/shard_map/ppermute | solution.py:214
  20.5 3.3 %collective-permute-start.2 = (bf16[4,16,128]{2,1,0:T(8,128)(2,1)S(1)}, bf16[4,16,128]{2,1,0:T(8,128)(2,1)S(1)}, u32[]{:S(2)}, u32[]{:S(2)}) collective-permute-start(bf16[4,16,128]{2,1,0:T(8,128)(2,1)S(1)} %get-tuple-element.12), channel_id=1, source_target_pairs={{0,3},{1,2},{2,1},{3,0},{4,7},{5,6},{6,5},{7,4},{8,11},{9,10},{10,... | collective-permute-start | bytes 49160 | tf_op jit(solution)/shard_map/ppermute | solution.py:214

commit v5 on v4

--- a/solution.py
+++ b/solution.py
@@ -79,6 +79,12 @@
     flat = arrived.reshape(arrived.shape[0] * arrived.shape[1], arrived.shape[2], arrived.shape[3])
     summed = correlate(own_rows, flat, spectra_len)
     return summed * (1.0 / math.sqrt(batch_count * spectra_len))
+
+
+def times_transposed(left, right):
+    return lax.dot_general(
+        left, right, (((1,), (1,)), ((), ())), preferred_element_type=jnp.float32
+    )
 
 
 def channelize_kernel(v_hbm, taps_hbm, dft_hbm, o_ref, v_ref, taps_ref, dft_ref, x_ref, f_ref, sems):
@@ -105,12 +111,15 @@
                     rows = x_ref[a, b, pl.ds(p * parts + h, spectra, stride=parts), :]
                     term = taps_ref[p : p + 1, lanes] * rows
                     total = term if total is None else total + term
-                f_ref[a, b * spectra : (b + 1) * spectra, lanes] = total.astype(jnp.bfloat16)
+                high = total.astype(jnp.bfloat16)
+                times = slice(b * spectra, (b + 1) * spectra)
+                f_ref[0, a, times, lanes] = high
+                f_ref[1, a, times, lanes] = (total - high.astype(jnp.float32)).astype(jnp.bfloat16)
     copy_dft.wait()
     for a in range(antennas):
-        spec = lax.dot_general(
-            dft_ref[...], f_ref[a], (((1,), (1,)), ((), ())), preferred_element_type=jnp.float32
-        )
+        spec = times_transposed(dft_ref[0], f_ref[0, a])
+        spec = spec + times_transposed(dft_ref[1], f_ref[0, a])
+        spec = spec + times_transposed(dft_ref[0], f_ref[1, a])
         o_ref[:, a, :, :] = spec.astype(jnp.bfloat16).reshape(
             o_ref.shape[0], o_ref.shape[2], o_ref.shape[3]
         )
@@ -135,9 +144,7 @@
         own = jnp.concatenate(re + im, axis=1).astype(jnp.bfloat16)
         turned = jnp.concatenate([-x for x in im] + re, axis=1).astype(jnp.bfloat16)
         both = jnp.concatenate([own, turned], axis=0)
-        prod = lax.dot_general(
-            own, both, (((1,), (1,)), ((), ())), preferred_element_type=jnp.float32
-        )
+        prod = times_transposed(own, both)
         vis[:, c, :, :] = (prod * scale).reshape(blocks, total // blocks, 2 * total)
     me = lax.axis_index("pair")
     for j in range(blocks):
@@ -164,7 +171,9 @@
     devices = groups * blocks
     channels = frame // 2 // devices
     total = devices * antennas
-    table = jnp.asarray(dft_table(frame // 2), jnp.bfloat16)
+    table = dft_table(frame // 2)
+    high = table.astype(jnp.bfloat16)
+    table = jnp.asarray(np.stack([high, (table - high.astype(np.float64)).astype(jnp.bfloat16)]))
     vmem = pl.BlockSpec(memory_space=VMEM)
     hbm = pl.BlockSpec(memory_space=pltpu.MemorySpace.HBM)
     sent = pl.pallas_call(
@@ -177,9 +186,9 @@
         scratch_shapes=[
             pltpu.VMEM((antennas, batches, length), jnp.bfloat16),
             pltpu.VMEM((taps, frame), jnp.float32),
-            pltpu.VMEM((frame, frame), jnp.bfloat16),
+            pltpu.VMEM((2, frame, frame), jnp.bfloat16),
             pltpu.VMEM((antennas, batches, length // LANES, LANES), jnp.float32),
-            pltpu.VMEM((antennas, batches * spectra, frame), jnp.bfloat16),
+            pltpu.VMEM((2, antennas, batches * spectra, frame), jnp.bfloat16),
             pltpu.SemaphoreType.DMA((antennas + 2,)),
         ],
         compiler_params=pltpu.CompilerParams(vmem_limit_bytes=LIMIT),

time: 24.8 us -> 25 us (level)
  no operation moved by 1% of the time
where the time goes in v5:
time: 25 us; the launch traced here: 24.9 us
  blocking collectives  17.7 us (71%)
  Pallas kernels  2.92 us (12%)
  waiting for transfers between devices  2.3 us (9%)
  starting transfers between devices  1.92 us (8%)
    all_to_all x1, blocking collectives, exchanged_shards(): turned = lax.all_to_all(sent, ('chan', 'pair'), 0, 0, tiled=True)  17.7 us
    ppermute x3, waiting for transfers between devices, exchanged_shards(): lax.ppermute(pieces[j], 'pair', [(i, i ^ j) for i in range(blocks)])  2.3 us
    ppermute x3, starting transfers between devices, exchanged_shards(): lax.ppermute(pieces[j], 'pair', [(i, i ^ j) for i in range(blocks)])  1.92 us
    pallas_call x1, Pallas kernels, exchanged_shards(): pl.pallas_call(channelize_kernel, out_shape=jax.ShapeDtypeStruct((devices...  1.77 us
    pallas_call x1, Pallas kernels, exchanged_shards(): pl.pallas_call(functools.partial(place_kernel, blocks), out_shape=jax.Sha...  0.8 us
  transfers between devices with their start and end apart: 3, of which 2 were waited for; matrix products, arithmetic and copies ran while one was open for 0% of the time, Pallas kernels for 0%

profile of v5, /device:TPU:0, one launch (start us, length us, event | category | flops | bytes accessed | tf_op | source)
XLA Modules:
  0.0 24.9 jit_solution(11656255946742621253)
XLA Ops:
  0.0 1.8 %channelize.1 = bf16[32,2,8,256]{3,2,1,0:T(8,128)(2,1)S(1)} custom-call(bf16[2,2,34560]{2,1,0:T(2,128)(2,1)} %bitcast.5, f32[8,256]{1,0:T(8,128)} %taps_hbm.1, bf16[2,256,256]{2,1,0:T(8,128)(2,1)} %constant.2.clone.dft_hbm), custom_call_target="tpu_custom_call" | custom-call | tf_op jit(solution)/shard_map/channelize/pallas_call | solution.py:179
  1.8 17.7 %all_to_all.5 = bf16[32,16,256]{2,1,0:T(8,128)(2,1)S(1)} all-to-all(bf16[32,16,256]{2,1,0:T(8,128)(2,1)S(1)} %bitcast.3), channel_id=1, replica_groups=mesh['chan'=8,'pair'=4] {'chan','pair'}, dimensions={0} | all-to-all | bytes 524288 | tf_op jit(solution)/shard_map/all_to_all | solution.py:198
  19.5 0.4 %correlate.1 = (f32[4,16,128]{2,1,0:T(8,128)S(1)}, f32[4,16,128]{2,1,0:T(8,128)S(1)}, bf16[4,16,128]{2,1,0:T(8,128)(2,1)S(1)}, bf16[4,16,128]{2,1,0:T(8,128)(2,1)S(1)}) custom-call(bf16[512,256]{1,0:T(8,128)(2,1)S(1)} %bitcast.4), custom_call_target="tpu_custom_call" | custom-call | tf_op jit(solution)/shard_map/correlate/pallas_call | solution.py:201
  19.8 0.1 collective-permute-start
  19.9 0.8 %collective-permute-start.1 = (bf16[4,16,128]{2,1,0:T(8,128)(2,1)S(1)}, bf16[4,16,128]{2,1,0:T(8,128)(2,1)S(1)}, u32[]{:S(2)}, u32[]{:S(2)}) collective-permute-start(bf16[4,16,128]{2,1,0:T(8,128)(2,1)S(1)} %get-tuple-element.11), channel_id=1, source_target_pairs={{0,2},{1,3},{2,0},{3,1},{4,6},{5,7},{6,4},{7,5},{8,10},{9,11},{10,... | collective-permute-start | bytes 49160 | tf_op jit(solution)/shard_map/ppermute | solution.py:223
  20.7 1.0 %collective-permute-start.2 = (bf16[4,16,128]{2,1,0:T(8,128)(2,1)S(1)}, bf16[4,16,128]{2,1,0:T(8,128)(2,1)S(1)}, u32[]{:S(2)}, u32[]{:S(2)}) collective-permute-start(bf16[4,16,128]{2,1,0:T(8,128)(2,1)S(1)} %get-tuple-element.12), channel_id=1, source_target_pairs={{0,3},{1,2},{2,1},{3,0},{4,7},{5,6},{6,5},{7,4},{8,11},{9,10},{10,... | collective-permute-start | bytes 49160 | tf_op jit(solution)/shard_map/ppermute | solution.py:223
  21.8 2.0 %collective-permute-done.1.refs_2_ = bf16[4,16,128]{2,1,0:T(8,128)(2,1)S(1)} collective-permute-done((bf16[4,16,128]{2,1,0:T(8,128)(2,1)S(1)}, bf16[4,16,128]{2,1,0:T(8,128)(2,1)S(1)}, u32[]{:S(2)}, u32[]{:S(2)}) %collective-permute-start.1) | collective-permute-done | bytes 16416 | tf_op jit(solution)/shard_map/ppermute | solution.py:223
  23.7 0.3 %collective-permute-done.2.refs_3_ = bf16[4,16,128]{2,1,0:T(8,128)(2,1)S(1)} collective-permute-done((bf16[4,16,128]{2,1,0:T(8,128)(2,1)S(1)}, bf16[4,16,128]{2,1,0:T(8,128)(2,1)S(1)}, u32[]{:S(2)}, u32[]{:S(2)}) %collective-permute-start.2) | collective-permute-done | bytes 16416 | tf_op jit(solution)/shard_map/ppermute | solution.py:223
  24.1 0.0 collective-permute-done.refs_1_
  24.1 0.8 %place.1 = f32[16,2,16,64]{3,2,1,0:T(8,128)} custom-call(f32[4,16,128]{2,1,0:T(8,128)S(1)} %get-tuple-element.9.refs_0_, f32[4,16,128]{2,1,0:T(8,128)S(1)} %collective-permute-done.refs_1_, bf16[4,16,128]{2,1,0:T(8,128)(2,1)S(1)} %collective-permute-done.1.refs_2_, bf16[4,16,128]{2,1,0:T(8,128)(2,1)S(1)} %collective-permute-done.2.refs_3_), custom_call_target="tpu_custom_call" | custom-call | tf_op jit(solution)/shard_map/place/pallas_call | solution.py:226
Async XLA Ops:
  19.8 4.2 %collective-permute-start = (f32[4,16,128]{2,1,0:T(8,128)S(1)}, f32[4,16,128]{2,1,0:T(8,128)S(1)}, u32[]{:S(2)}, u32[]{:S(2)}) collective-permute-start(f32[4,16,128]{2,1,0:T(8,128)S(1)} %get-tuple-element.10), channel_id=1, source_target_pairs={{0,1},{1,0},{2,3},{3,2},{4,5},{5,4},{6,7},{7,6},{8,9},{9,8},{10,11... | collective-permute-start | bytes 98312 | tf_op jit(solution)/shard_map/ppermute | solution.py:223
  19.9 3.8 %collective-permute-start.1 = (bf16[4,16,128]{2,1,0:T(8,128)(2,1)S(1)}, bf16[4,16,128]{2,1,0:T(8,128)(2,1)S(1)}, u32[]{:S(2)}, u32[]{:S(2)}) collective-permute-start(bf16[4,16,128]{2,1,0:T(8,128)(2,1)S(1)} %get-tuple-element.11), channel_id=1, source_target_pairs={{0,2},{1,3},{2,0},{3,1},{4,6},{5,7},{6,4},{7,5},{8,10},{9,11},{10,... | collective-permute-start | bytes 49160 | tf_op jit(solution)/shard_map/ppermute | solution.py:223
  20.7 3.3 %collective-permute-start.2 = (bf16[4,16,128]{2,1,0:T(8,128)(2,1)S(1)}, bf16[4,16,128]{2,1,0:T(8,128)(2,1)S(1)}, u32[]{:S(2)}, u32[]{:S(2)}) collective-permute-start(bf16[4,16,128]{2,1,0:T(8,128)(2,1)S(1)} %get-tuple-element.12), channel_id=1, source_target_pairs={{0,3},{1,2},{2,1},{3,0},{4,7},{5,6},{6,5},{7,4},{8,11},{9,10},{10,... | collective-permute-start | bytes 49160 | tf_op jit(solution)/shard_map/ppermute | solution.py:223

commit v6 on v5

--- a/solution.py
+++ b/solution.py
@@ -8,6 +8,7 @@
 from jax.experimental import pallas as pl
 from jax.experimental.pallas import tpu as pltpu
 from jax.sharding import PartitionSpec as P
+
 
 LANES = 128
 LIMIT = 16 * 2**20
@@ -219,10 +220,11 @@
         compiler_params=pltpu.CompilerParams(vmem_limit_bytes=LIMIT),
         name="correlate",
     )(turned.reshape(devices * antennas * 2 * channels, batches * spectra))
-    arrived = [pieces[0]] + [
-        lax.ppermute(pieces[j], "pair", [(i, i ^ j) for i in range(blocks)])
-        for j in range(1, blocks)
-    ]
+    arrived = [pieces[0]]
+    for j in range(1, blocks):
+        arrived.append(
+            lax.ppermute(pieces[j], "pair", [(i, i ^ j) for i in range(blocks)])
+        )
     return pl.pallas_call(
         functools.partial(place_kernel, blocks),
         out_shape=jax.ShapeDtypeStruct(

time: 25 us -> 25 us (level)
  no operation moved by 1% of the time
where the time goes in v6:
time: 25 us; the launch traced here: 24.9 us
  blocking collectives  17.7 us (71%)
  Pallas kernels  2.92 us (12%)
  waiting for transfers between devices  2.3 us (9%)
  starting transfers between devices  1.92 us (8%)
    all_to_all x1, blocking collectives, exchanged_shards(): turned = lax.all_to_all(sent, ('chan', 'pair'), 0, 0, tiled=True)  17.7 us
    ppermute x3, waiting for transfers between devices, exchanged_shards(): lax.ppermute(pieces[j], 'pair', [(i, i ^ j) for i in range(blocks)])  2.3 us
    ppermute x3, starting transfers between devices, exchanged_shards(): lax.ppermute(pieces[j], 'pair', [(i, i ^ j) for i in range(blocks)])  1.92 us
    pallas_call x1, Pallas kernels, exchanged_shards(): pl.pallas_call(channelize_kernel, out_shape=jax.ShapeDtypeStruct((devices...  1.77 us
    pallas_call x1, Pallas kernels, exchanged_shards(): pl.pallas_call(functools.partial(place_kernel, blocks), out_shape=jax.Sha...  0.8 us
  transfers between devices with their start and end apart: 3, of which 2 were waited for; matrix products, arithmetic and copies ran while one was open for 0% of the time, Pallas kernels for 0%

profile of v6, /device:TPU:0, one launch (start us, length us, event | category | flops | bytes accessed | tf_op | source)
XLA Modules:
  0.0 24.9 jit_solution(11656255946742621253)
XLA Ops:
  0.0 1.8 %channelize.1 = bf16[32,2,8,256]{3,2,1,0:T(8,128)(2,1)S(1)} custom-call(bf16[2,2,34560]{2,1,0:T(2,128)(2,1)} %bitcast.5, f32[8,256]{1,0:T(8,128)} %taps_hbm.1, bf16[2,256,256]{2,1,0:T(8,128)(2,1)} %constant.2.clone.dft_hbm), custom_call_target="tpu_custom_call" | custom-call | tf_op jit(solution)/shard_map/channelize/pallas_call | solution.py:180
  1.8 17.7 %all_to_all.5 = bf16[32,16,256]{2,1,0:T(8,128)(2,1)S(1)} all-to-all(bf16[32,16,256]{2,1,0:T(8,128)(2,1)S(1)} %bitcast.3), channel_id=1, replica_groups=mesh['chan'=8,'pair'=4] {'chan','pair'}, dimensions={0} | all-to-all | bytes 524288 | tf_op jit(solution)/shard_map/all_to_all | solution.py:199
  19.5 0.4 %correlate.1 = (f32[4,16,128]{2,1,0:T(8,128)S(1)}, f32[4,16,128]{2,1,0:T(8,128)S(1)}, bf16[4,16,128]{2,1,0:T(8,128)(2,1)S(1)}, bf16[4,16,128]{2,1,0:T(8,128)(2,1)S(1)}) custom-call(bf16[512,256]{1,0:T(8,128)(2,1)S(1)} %bitcast.4), custom_call_target="tpu_custom_call" | custom-call | tf_op jit(solution)/shard_map/correlate/pallas_call | solution.py:202
  19.8 0.1 collective-permute-start
  19.9 0.8 %collective-permute-start.1 = (bf16[4,16,128]{2,1,0:T(8,128)(2,1)S(1)}, bf16[4,16,128]{2,1,0:T(8,128)(2,1)S(1)}, u32[]{:S(2)}, u32[]{:S(2)}) collective-permute-start(bf16[4,16,128]{2,1,0:T(8,128)(2,1)S(1)} %get-tuple-element.11), channel_id=1, source_target_pairs={{0,2},{1,3},{2,0},{3,1},{4,6},{5,7},{6,4},{7,5},{8,10},{9,11},{10,... | collective-permute-start | bytes 49160 | tf_op jit(solution)/shard_map/ppermute | solution.py:226
  20.7 1.0 %collective-permute-start.2 = (bf16[4,16,128]{2,1,0:T(8,128)(2,1)S(1)}, bf16[4,16,128]{2,1,0:T(8,128)(2,1)S(1)}, u32[]{:S(2)}, u32[]{:S(2)}) collective-permute-start(bf16[4,16,128]{2,1,0:T(8,128)(2,1)S(1)} %get-tuple-element.12), channel_id=1, source_target_pairs={{0,3},{1,2},{2,1},{3,0},{4,7},{5,6},{6,5},{7,4},{8,11},{9,10},{10,... | collective-permute-start | bytes 49160 | tf_op jit(solution)/shard_map/ppermute | solution.py:226
  21.8 2.0 %collective-permute-done.1.refs_2_ = bf16[4,16,128]{2,1,0:T(8,128)(2,1)S(1)} collective-permute-done((bf16[4,16,128]{2,1,0:T(8,128)(2,1)S(1)}, bf16[4,16,128]{2,1,0:T(8,128)(2,1)S(1)}, u32[]{:S(2)}, u32[]{:S(2)}) %collective-permute-start.1) | collective-permute-done | bytes 16416 | tf_op jit(solution)/shard_map/ppermute | solution.py:226
  23.7 0.3 %collective-permute-done.2.refs_3_ = bf16[4,16,128]{2,1,0:T(8,128)(2,1)S(1)} collective-permute-done((bf16[4,16,128]{2,1,0:T(8,128)(2,1)S(1)}, bf16[4,16,128]{2,1,0:T(8,128)(2,1)S(1)}, u32[]{:S(2)}, u32[]{:S(2)}) %collective-permute-start.2) | collective-permute-done | bytes 16416 | tf_op jit(solution)/shard_map/ppermute | solution.py:226
  24.1 0.0 collective-permute-done.refs_1_
  24.1 0.8 %place.1 = f32[16,2,16,64]{3,2,1,0:T(8,128)} custom-call(f32[4,16,128]{2,1,0:T(8,128)S(1)} %get-tuple-element.9.refs_0_, f32[4,16,128]{2,1,0:T(8,128)S(1)} %collective-permute-done.refs_1_, bf16[4,16,128]{2,1,0:T(8,128)(2,1)S(1)} %collective-permute-done.1.refs_2_, bf16[4,16,128]{2,1,0:T(8,128)(2,1)S(1)} %collective-permute-done.2.refs_3_), custom_call_target="tpu_custom_call" | custom-call | tf_op jit(solution)/shard_map/place/pallas_call | solution.py:228
Async XLA Ops:
  19.8 4.2 %collective-permute-start = (f32[4,16,128]{2,1,0:T(8,128)S(1)}, f32[4,16,128]{2,1,0:T(8,128)S(1)}, u32[]{:S(2)}, u32[]{:S(2)}) collective-permute-start(f32[4,16,128]{2,1,0:T(8,128)S(1)} %get-tuple-element.10), channel_id=1, source_target_pairs={{0,1},{1,0},{2,3},{3,2},{4,5},{5,4},{6,7},{7,6},{8,9},{9,8},{10,11... | collective-permute-start | bytes 98312 | tf_op jit(solution)/shard_map/ppermute | solution.py:226
  19.9 3.8 %collective-permute-start.1 = (bf16[4,16,128]{2,1,0:T(8,128)(2,1)S(1)}, bf16[4,16,128]{2,1,0:T(8,128)(2,1)S(1)}, u32[]{:S(2)}, u32[]{:S(2)}) collective-permute-start(bf16[4,16,128]{2,1,0:T(8,128)(2,1)S(1)} %get-tuple-element.11), channel_id=1, source_target_pairs={{0,2},{1,3},{2,0},{3,1},{4,6},{5,7},{6,4},{7,5},{8,10},{9,11},{10,... | collective-permute-start | bytes 49160 | tf_op jit(solution)/shard_map/ppermute | solution.py:226
  20.7 3.3 %collective-permute-start.2 = (bf16[4,16,128]{2,1,0:T(8,128)(2,1)S(1)}, bf16[4,16,128]{2,1,0:T(8,128)(2,1)S(1)}, u32[]{:S(2)}, u32[]{:S(2)}) collective-permute-start(bf16[4,16,128]{2,1,0:T(8,128)(2,1)S(1)} %get-tuple-element.12), channel_id=1, source_target_pairs={{0,3},{1,2},{2,1},{3,0},{4,7},{5,6},{6,5},{7,4},{8,11},{9,10},{10,... | collective-permute-start | bytes 49160 | tf_op jit(solution)/shard_map/ppermute | solution.py:226

commit v7 on v6

--- a/solution.py
+++ b/solution.py
@@ -88,7 +88,12 @@
     )
 
 
-def channelize_kernel(v_hbm, taps_hbm, dft_hbm, o_ref, v_ref, taps_ref, dft_ref, x_ref, f_ref, sems):
+def transformed(dft_ref, high, low):
+    total = times_transposed(dft_ref[0], high) + times_transposed(dft_ref[1], high)
+    return total + times_transposed(dft_ref[0], low)
+
+
+def channelize_kernel(v_hbm, taps_hbm, dft_hbm, o_ref, v_ref, taps_ref, dft_ref, x_ref, sems):
     antennas, batches, length = v_ref.shape
     taps, frame = taps_ref.shape
     copies = [pltpu.make_async_copy(v_hbm.at[a], v_ref.at[a], sems.at[a]) for a in range(antennas)]
@@ -99,12 +104,19 @@
     copy_taps.wait()
     parts = frame // LANES
     spectra = length // frame - taps + 1
+    spec = []
     for a in range(antennas):
         copies[a].wait()
+        if a == 1 or antennas == 1:
+            copy_dft.wait()
+        if a > 0:
+            spec.append(transformed(dft_ref, *split))
         samples = v_ref[a].astype(jnp.float32)
         for b in range(batches):
             x_ref[a, b] = samples[b].reshape(length // LANES, LANES)
+        filtered = []
         for b in range(batches):
+            row = []
             for h in range(parts):
                 lanes = slice(h * LANES, (h + 1) * LANES)
                 total = None
@@ -113,15 +125,15 @@
                     term = taps_ref[p : p + 1, lanes] * rows
                     total = term if total is None else total + term
                 high = total.astype(jnp.bfloat16)
-                times = slice(b * spectra, (b + 1) * spectra)
-                f_ref[0, a, times, lanes] = high
-                f_ref[1, a, times, lanes] = (total - high.astype(jnp.float32)).astype(jnp.bfloat16)
-    copy_dft.wait()
+                row.append((high, (total - high.astype(jnp.float32)).astype(jnp.bfloat16)))
+            filtered.append(row)
+        split = [
+            jnp.concatenate([jnp.concatenate([x[n] for x in row], axis=1) for row in filtered], axis=0)
+            for n in range(2)
+        ]
+    spec.append(transformed(dft_ref, *split))
     for a in range(antennas):
-        spec = times_transposed(dft_ref[0], f_ref[0, a])
-        spec = spec + times_transposed(dft_ref[1], f_ref[0, a])
-        spec = spec + times_transposed(dft_ref[0], f_ref[1, a])
-        o_ref[:, a, :, :] = spec.astype(jnp.bfloat16).reshape(
+        o_ref[:, a, :, :] = spec[a].astype(jnp.bfloat16).reshape(
             o_ref.shape[0], o_ref.shape[2], o_ref.shape[3]
         )
 
@@ -189,7 +201,6 @@
             pltpu.VMEM((taps, frame), jnp.float32),
             pltpu.VMEM((2, frame, frame), jnp.bfloat16),
             pltpu.VMEM((antennas, batches, length // LANES, LANES), jnp.float32),
-            pltpu.VMEM((2, antennas, batches * spectra, frame), jnp.bfloat16),
             pltpu.SemaphoreType.DMA((antennas + 2,)),
         ],
         compiler_params=pltpu.CompilerParams(vmem_limit_bytes=LIMIT),

time: 25 us -> 25 us (level)
  no operation moved by 1% of the time
where the time goes in v7:
time: 25 us; the launch traced here: 24.8 us
  blocking collectives  17.7 us (71%)
  Pallas kernels  2.84 us (11%)
  waiting for transfers between devices  2.3 us (9%)
  starting transfers between devices  1.92 us (8%)
    all_to_all x1, blocking collectives, exchanged_shards(): turned = lax.all_to_all(sent, ('chan', 'pair'), 0, 0, tiled=True)  17.7 us
    ppermute x3, waiting for transfers between devices, exchanged_shards(): lax.ppermute(pieces[j], 'pair', [(i, i ^ j) for i in range(blocks)])  2.3 us
    ppermute x3, starting transfers between devices, exchanged_shards(): lax.ppermute(pieces[j], 'pair', [(i, i ^ j) for i in range(blocks)])  1.92 us
    pallas_call x1, Pallas kernels, exchanged_shards(): pl.pallas_call(channelize_kernel, out_shape=jax.ShapeDtypeStruct((devices...  1.69 us
    pallas_call x1, Pallas kernels, exchanged_shards(): pl.pallas_call(functools.partial(place_kernel, blocks), out_shape=jax.Sha...  0.8 us
  transfers between devices with their start and end apart: 3, of which 2 were waited for; matrix products, arithmetic and copies ran while one was open for 0% of the time, Pallas kernels for 0%

profile of v7, /device:TPU:0, one launch (start us, length us, event | category | flops | bytes accessed | tf_op | source)
XLA Modules:
  0.0 24.8 jit_solution(5611459229881376356)
XLA Ops:
  0.0 1.7 %channelize.1 = bf16[32,2,8,256]{3,2,1,0:T(8,128)(2,1)S(1)} custom-call(bf16[2,2,34560]{2,1,0:T(2,128)(2,1)} %bitcast.5, f32[8,256]{1,0:T(8,128)} %taps_hbm.1, bf16[2,256,256]{2,1,0:T(8,128)(2,1)} %constant.2.clone.dft_hbm), custom_call_target="tpu_custom_call" | custom-call | tf_op jit(solution)/shard_map/channelize/pallas_call | solution.py:192
  1.7 17.7 %all_to_all.5 = bf16[32,16,256]{2,1,0:T(8,128)(2,1)S(1)} all-to-all(bf16[32,16,256]{2,1,0:T(8,128)(2,1)S(1)} %bitcast.3), channel_id=1, replica_groups=mesh['chan'=8,'pair'=4] {'chan','pair'}, dimensions={0} | all-to-all | bytes 524288 | tf_op jit(solution)/shard_map/all_to_all | solution.py:210
  19.4 0.4 %correlate.1 = (f32[4,16,128]{2,1,0:T(8,128)S(1)}, f32[4,16,128]{2,1,0:T(8,128)S(1)}, bf16[4,16,128]{2,1,0:T(8,128)(2,1)S(1)}, bf16[4,16,128]{2,1,0:T(8,128)(2,1)S(1)}) custom-call(bf16[512,256]{1,0:T(8,128)(2,1)S(1)} %bitcast.4), custom_call_target="tpu_custom_call" | custom-call | tf_op jit(solution)/shard_map/correlate/pallas_call | solution.py:213
  19.8 0.1 collective-permute-start
  19.8 0.8 %collective-permute-start.1 = (bf16[4,16,128]{2,1,0:T(8,128)(2,1)S(1)}, bf16[4,16,128]{2,1,0:T(8,128)(2,1)S(1)}, u32[]{:S(2)}, u32[]{:S(2)}) collective-permute-start(bf16[4,16,128]{2,1,0:T(8,128)(2,1)S(1)} %get-tuple-element.11), channel_id=1, source_target_pairs={{0,2},{1,3},{2,0},{3,1},{4,6},{5,7},{6,4},{7,5},{8,10},{9,11},{10,... | collective-permute-start | bytes 49160 | tf_op jit(solution)/shard_map/ppermute | solution.py:237
  20.7 1.0 %collective-permute-start.2 = (bf16[4,16,128]{2,1,0:T(8,128)(2,1)S(1)}, bf16[4,16,128]{2,1,0:T(8,128)(2,1)S(1)}, u32[]{:S(2)}, u32[]{:S(2)}) collective-permute-start(bf16[4,16,128]{2,1,0:T(8,128)(2,1)S(1)} %get-tuple-element.12), channel_id=1, source_target_pairs={{0,3},{1,2},{2,1},{3,0},{4,7},{5,6},{6,5},{7,4},{8,11},{9,10},{10,... | collective-permute-start | bytes 49160 | tf_op jit(solution)/shard_map/ppermute | solution.py:237
  21.7 2.0 %collective-permute-done.1.refs_2_ = bf16[4,16,128]{2,1,0:T(8,128)(2,1)S(1)} collective-permute-done((bf16[4,16,128]{2,1,0:T(8,128)(2,1)S(1)}, bf16[4,16,128]{2,1,0:T(8,128)(2,1)S(1)}, u32[]{:S(2)}, u32[]{:S(2)}) %collective-permute-start.1) | collective-permute-done | bytes 16416 | tf_op jit(solution)/shard_map/ppermute | solution.py:237
  23.6 0.3 %collective-permute-done.2.refs_3_ = bf16[4,16,128]{2,1,0:T(8,128)(2,1)S(1)} collective-permute-done((bf16[4,16,128]{2,1,0:T(8,128)(2,1)S(1)}, bf16[4,16,128]{2,1,0:T(8,128)(2,1)S(1)}, u32[]{:S(2)}, u32[]{:S(2)}) %collective-permute-start.2) | collective-permute-done | bytes 16416 | tf_op jit(solution)/shard_map/ppermute | solution.py:237
  24.0 0.0 collective-permute-done.refs_1_
  24.0 0.8 %place.1 = f32[16,2,16,64]{3,2,1,0:T(8,128)} custom-call(f32[4,16,128]{2,1,0:T(8,128)S(1)} %get-tuple-element.9.refs_0_, f32[4,16,128]{2,1,0:T(8,128)S(1)} %collective-permute-done.refs_1_, bf16[4,16,128]{2,1,0:T(8,128)(2,1)S(1)} %collective-permute-done.1.refs_2_, bf16[4,16,128]{2,1,0:T(8,128)(2,1)S(1)} %collective-permute-done.2.refs_3_), custom_call_target="tpu_custom_call" | custom-call | tf_op jit(solution)/shard_map/place/pallas_call | solution.py:239
Async XLA Ops:
  19.8 4.2 %collective-permute-start = (f32[4,16,128]{2,1,0:T(8,128)S(1)}, f32[4,16,128]{2,1,0:T(8,128)S(1)}, u32[]{:S(2)}, u32[]{:S(2)}) collective-permute-start(f32[4,16,128]{2,1,0:T(8,128)S(1)} %get-tuple-element.10), channel_id=1, source_target_pairs={{0,1},{1,0},{2,3},{3,2},{4,5},{5,4},{6,7},{7,6},{8,9},{9,8},{10,11... | collective-permute-start | bytes 98312 | tf_op jit(solution)/shard_map/ppermute | solution.py:237
  19.8 3.8 %collective-permute-start.1 = (bf16[4,16,128]{2,1,0:T(8,128)(2,1)S(1)}, bf16[4,16,128]{2,1,0:T(8,128)(2,1)S(1)}, u32[]{:S(2)}, u32[]{:S(2)}) collective-permute-start(bf16[4,16,128]{2,1,0:T(8,128)(2,1)S(1)} %get-tuple-element.11), channel_id=1, source_target_pairs={{0,2},{1,3},{2,0},{3,1},{4,6},{5,7},{6,4},{7,5},{8,10},{9,11},{10,... | collective-permute-start | bytes 49160 | tf_op jit(solution)/shard_map/ppermute | solution.py:237
  20.7 3.3 %collective-permute-start.2 = (bf16[4,16,128]{2,1,0:T(8,128)(2,1)S(1)}, bf16[4,16,128]{2,1,0:T(8,128)(2,1)S(1)}, u32[]{:S(2)}, u32[]{:S(2)}) collective-permute-start(bf16[4,16,128]{2,1,0:T(8,128)(2,1)S(1)} %get-tuple-element.12), channel_id=1, source_target_pairs={{0,3},{1,2},{2,1},{3,0},{4,7},{5,6},{6,5},{7,4},{8,11},{9,10},{10,... | collective-permute-start | bytes 49160 | tf_op jit(solution)/shard_map/ppermute | solution.py:237

commit v8 on v7

--- a/solution.py
+++ b/solution.py
@@ -151,13 +151,16 @@
                 scr[t, (q * groups + g) * rows : (q * groups + g + 1) * rows, :] = src[
                     :, t * LANES : (t + 1) * LANES
                 ]
+    gathered = []
     for c in range(channels):
         re = [scr[t, pl.ds(2 * c, total, stride=2 * channels), :] for t in range(parts)]
         im = [scr[t, pl.ds(2 * c + 1, total, stride=2 * channels), :] for t in range(parts)]
         own = jnp.concatenate(re + im, axis=1).astype(jnp.bfloat16)
         turned = jnp.concatenate([-x for x in im] + re, axis=1).astype(jnp.bfloat16)
-        both = jnp.concatenate([own, turned], axis=0)
-        prod = times_transposed(own, both)
+        gathered.append((own, jnp.concatenate([own, turned], axis=0)))
+    for c, (own, both) in enumerate(gathered):
+        prod = times_transposed(own[:, :width], both[:, :width])
+        prod = prod + times_transposed(own[:, width:], both[:, width:])
         vis[:, c, :, :] = (prod * scale).reshape(blocks, total // blocks, 2 * total)
     me = lax.axis_index("pair")
     for j in range(blocks):

time: 25 us -> 24.9 us (level)
  no operation moved by 1% of the time
where the time goes in v8:
time: 24.9 us; the launch traced here: 24.8 us
  blocking collectives  17.7 us (71%)
  Pallas kernels  2.83 us (11%)
  waiting for transfers between devices  2.3 us (9%)
  starting transfers between devices  1.92 us (8%)
    all_to_all x1, blocking collectives, exchanged_shards(): turned = lax.all_to_all(sent, ('chan', 'pair'), 0, 0, tiled=True)  17.7 us
    ppermute x3, waiting for transfers between devices, exchanged_shards(): lax.ppermute(pieces[j], 'pair', [(i, i ^ j) for i in range(blocks)])  2.3 us
    ppermute x3, starting transfers between devices, exchanged_shards(): lax.ppermute(pieces[j], 'pair', [(i, i ^ j) for i in range(blocks)])  1.92 us
    pallas_call x1, Pallas kernels, exchanged_shards(): pl.pallas_call(channelize_kernel, out_shape=jax.ShapeDtypeStruct((devices...  1.69 us
    pallas_call x1, Pallas kernels, exchanged_shards(): pl.pallas_call(functools.partial(place_kernel, blocks), out_shape=jax.Sha...  0.8 us
  transfers between devices with their start and end apart: 3, of which 2 were waited for; matrix products, arithmetic and copies ran while one was open for 0% of the time, Pallas kernels for 0%

profile of v8, /device:TPU:0, one launch (start us, length us, event | category | flops | bytes accessed | tf_op | source)
XLA Modules:
  0.0 24.8 jit_solution(15401566846072014964)
XLA Ops:
  0.0 1.7 %channelize.1 = bf16[32,2,8,256]{3,2,1,0:T(8,128)(2,1)S(1)} custom-call(bf16[2,2,34560]{2,1,0:T(2,128)(2,1)} %bitcast.5, f32[8,256]{1,0:T(8,128)} %taps_hbm.1, bf16[2,256,256]{2,1,0:T(8,128)(2,1)} %constant.2.clone.dft_hbm), custom_call_target="tpu_custom_call" | custom-call | tf_op jit(solution)/shard_map/channelize/pallas_call | solution.py:195
  1.7 17.7 %all_to_all.5 = bf16[32,16,256]{2,1,0:T(8,128)(2,1)S(1)} all-to-all(bf16[32,16,256]{2,1,0:T(8,128)(2,1)S(1)} %bitcast.3), channel_id=1, replica_groups=mesh['chan'=8,'pair'=4] {'chan','pair'}, dimensions={0} | all-to-all | bytes 524288 | tf_op jit(solution)/shard_map/all_to_all | solution.py:213
  19.4 0.3 %correlate.1 = (f32[4,16,128]{2,1,0:T(8,128)S(1)}, f32[4,16,128]{2,1,0:T(8,128)S(1)}, bf16[4,16,128]{2,1,0:T(8,128)(2,1)S(1)}, bf16[4,16,128]{2,1,0:T(8,128)(2,1)S(1)}) custom-call(bf16[512,256]{1,0:T(8,128)(2,1)S(1)} %bitcast.4), custom_call_target="tpu_custom_call" | custom-call | tf_op jit(solution)/shard_map/correlate/pallas_call | solution.py:216
  19.8 0.1 collective-permute-start
  19.8 0.8 %collective-permute-start.1 = (bf16[4,16,128]{2,1,0:T(8,128)(2,1)S(1)}, bf16[4,16,128]{2,1,0:T(8,128)(2,1)S(1)}, u32[]{:S(2)}, u32[]{:S(2)}) collective-permute-start(bf16[4,16,128]{2,1,0:T(8,128)(2,1)S(1)} %get-tuple-element.11), channel_id=1, source_target_pairs={{0,2},{1,3},{2,0},{3,1},{4,6},{5,7},{6,4},{7,5},{8,10},{9,11},{10,... | collective-permute-start | bytes 49160 | tf_op jit(solution)/shard_map/ppermute | solution.py:240
  20.6 1.0 %collective-permute-start.2 = (bf16[4,16,128]{2,1,0:T(8,128)(2,1)S(1)}, bf16[4,16,128]{2,1,0:T(8,128)(2,1)S(1)}, u32[]{:S(2)}, u32[]{:S(2)}) collective-permute-start(bf16[4,16,128]{2,1,0:T(8,128)(2,1)S(1)} %get-tuple-element.12), channel_id=1, source_target_pairs={{0,3},{1,2},{2,1},{3,0},{4,7},{5,6},{6,5},{7,4},{8,11},{9,10},{10,... | collective-permute-start | bytes 49160 | tf_op jit(solution)/shard_map/ppermute | solution.py:240
  21.7 2.0 %collective-permute-done.1.refs_2_ = bf16[4,16,128]{2,1,0:T(8,128)(2,1)S(1)} collective-permute-done((bf16[4,16,128]{2,1,0:T(8,128)(2,1)S(1)}, bf16[4,16,128]{2,1,0:T(8,128)(2,1)S(1)}, u32[]{:S(2)}, u32[]{:S(2)}) %collective-permute-start.1) | collective-permute-done | bytes 16416 | tf_op jit(solution)/shard_map/ppermute | solution.py:240
  23.6 0.3 %collective-permute-done.2.refs_3_ = bf16[4,16,128]{2,1,0:T(8,128)(2,1)S(1)} collective-permute-done((bf16[4,16,128]{2,1,0:T(8,128)(2,1)S(1)}, bf16[4,16,128]{2,1,0:T(8,128)(2,1)S(1)}, u32[]{:S(2)}, u32[]{:S(2)}) %collective-permute-start.2) | collective-permute-done | bytes 16416 | tf_op jit(solution)/shard_map/ppermute | solution.py:240
  24.0 0.0 collective-permute-done.refs_1_
  24.0 0.8 %place.1 = f32[16,2,16,64]{3,2,1,0:T(8,128)} custom-call(f32[4,16,128]{2,1,0:T(8,128)S(1)} %get-tuple-element.9.refs_0_, f32[4,16,128]{2,1,0:T(8,128)S(1)} %collective-permute-done.refs_1_, bf16[4,16,128]{2,1,0:T(8,128)(2,1)S(1)} %collective-permute-done.1.refs_2_, bf16[4,16,128]{2,1,0:T(8,128)(2,1)S(1)} %collective-permute-done.2.refs_3_), custom_call_target="tpu_custom_call" | custom-call | tf_op jit(solution)/shard_map/place/pallas_call | solution.py:242
Async XLA Ops:
  19.8 4.2 %collective-permute-start = (f32[4,16,128]{2,1,0:T(8,128)S(1)}, f32[4,16,128]{2,1,0:T(8,128)S(1)}, u32[]{:S(2)}, u32[]{:S(2)}) collective-permute-start(f32[4,16,128]{2,1,0:T(8,128)S(1)} %get-tuple-element.10), channel_id=1, source_target_pairs={{0,1},{1,0},{2,3},{3,2},{4,5},{5,4},{6,7},{7,6},{8,9},{9,8},{10,11... | collective-permute-start | bytes 98312 | tf_op jit(solution)/shard_map/ppermute | solution.py:240
  19.8 3.8 %collective-permute-start.1 = (bf16[4,16,128]{2,1,0:T(8,128)(2,1)S(1)}, bf16[4,16,128]{2,1,0:T(8,128)(2,1)S(1)}, u32[]{:S(2)}, u32[]{:S(2)}) collective-permute-start(bf16[4,16,128]{2,1,0:T(8,128)(2,1)S(1)} %get-tuple-element.11), channel_id=1, source_target_pairs={{0,2},{1,3},{2,0},{3,1},{4,6},{5,7},{6,4},{7,5},{8,10},{9,11},{10,... | collective-permute-start | bytes 49160 | tf_op jit(solution)/shard_map/ppermute | solution.py:240
  20.6 3.3 %collective-permute-start.2 = (bf16[4,16,128]{2,1,0:T(8,128)(2,1)S(1)}, bf16[4,16,128]{2,1,0:T(8,128)(2,1)S(1)}, u32[]{:S(2)}, u32[]{:S(2)}) collective-permute-start(bf16[4,16,128]{2,1,0:T(8,128)(2,1)S(1)} %get-tuple-element.12), channel_id=1, source_target_pairs={{0,3},{1,2},{2,1},{3,0},{4,7},{5,6},{6,5},{7,4},{8,11},{9,10},{10,... | collective-permute-start | bytes 49160 | tf_op jit(solution)/shard_map/ppermute | solution.py:240
